TPU v7x, 128 devices: a whole 4x4x4 slice. The times are simulated.
128 devices in a mesh: ctx: 16 (over y, x_lo, core), head: 8 (over z, x_hi).
Axes of the slice: x: 4 (x_hi: 2, x_lo: 2; x = x_hi * 2 + x_lo), y: 4, z: 4, core: 2. Of those that a mesh axis runs over, the one named last changes fastest.
Arguments:
- activations: bfloat16 [32768, 4096], P('ctx', 'head'), may hold values from -80 to 80
- query_grad: bfloat16 [32768, 4096], P('ctx', 'head'), may hold values from -80 to 80
- example_ids: int32 [32768], P('ctx'), may hold values from 0 to 1, as said below
- band_coefs: bfloat16 [64], replicated, may hold values from 0.049804688 to 1
- noise_history: bfloat16 [64, 4096, 4096], P(None, ('ctx', 'head')), may hold values from -4 to 4
- momentum: float32 [4096, 4096], P(('ctx', 'head')), may hold values from -6 to 6
Outputs:
- momentum_new: float32 [4096, 4096], P(('ctx', 'head'))
- update: bfloat16 [4096, 4096], P('ctx', 'head')
Inputs may be any that keep to these rules, and one draw needn't show every extreme that they name: `example_ids`: example 0's tokens come first, then example 1's; each example holds a quarter or more of the 32768 tokens.
All inputs are finite; a program needn't handle non-finite values.
Results may differ from a plain program's by a relative error of at most 0.0085.
Values may be sent and summed in bfloat16 or wider, within the bound.
No kernel may reach another device: no remote copies, remote signals or barrier semaphores. Data moves between devices by JAX's collectives and lax.ppermute only.
A program may use at most 128 MiB of HBM per device.

v0:
```python
import math

import jax
import jax.numpy as jnp
from jax import lax
from jax.experimental import pallas as pl
from jax.experimental.pallas import tpu as pltpu
from jax.sharding import PartitionSpec as P


clip_scale = 1.0
momentum_decay = 0.9
noise_weight = 0.8

BOTH = ("ctx", "head")
NY, NXL, NCORE, NZ, NXH = 4, 2, 2, 4, 2
CHUNKS = (160, 96)
TOKEN_BLOCK = 1024
SPLIT = 2


def lin(y, xl, core, z, xh):
    return ((y * NXL + xl) * NCORE + core) * (NZ * NXH) + z * NXH + xh


def permute(value, move):
    pairs = []
    for y in range(NY):
        for xl in range(NXL):
            for core in range(NCORE):
                for z in range(NZ):
                    for xh in range(NXH):
                        pairs.append((lin(y, xl, core, z, xh), lin(*move(y, xl, core, z, xh))))
    return lax.ppermute(value, BOTH, pairs)


def swap_core(value):
    return permute(value, lambda y, xl, core, z, xh: (y, xl, 1 - core, z, xh))


def swap_xh(value):
    return permute(value, lambda y, xl, core, z, xh: (y, xl, core, z, 1 - xh))


def swap_xl(value):
    return permute(value, lambda y, xl, core, z, xh: (y, 1 - xl, core, z, xh))


def gather_x(value):
    def move(y, xl, core, z, xh):
        to = {0: 2, 1: 0, 2: 3, 3: 1}[NXL * xh + xl]
        return y, to % NXL, core, z, to // NXL

    return permute(value, move)


def cross_x(value):
    def move(y, xl, core, z, xh):
        to = {0: 3, 1: 2, 2: 1, 3: 0}[NXL * xh + xl]
        return y, to % NXL, core, z, to // NXL

    return permute(value, move)


def shift_z(value, step):
    return permute(value, lambda y, xl, core, z, xh: (y, xl, core, (z + step) % NZ, xh))


def shift_y(value, step):
    return permute(value, lambda y, xl, core, z, xh: ((y + step) % NY, xl, core, z, xh))


def turn_kernel(core, keep, give, *outs):
    kept, given = keep[...].T, give[...].T
    start = 0
    for i, rows in enumerate(CHUNKS):
        outs[2 * i][...] = kept[start : start + rows]
        outs[2 * i + 1][...] = given[start : start + rows]
        start += rows


def turn(core, activations):
    tokens, width = activations.shape
    half = width // NCORE
    block = 1024
    shapes, specs = [], []
    for rows in CHUNKS:
        for _ in range(2):
            shapes.append(jax.ShapeDtypeStruct((rows, tokens), activations.dtype))
            specs.append(pl.BlockSpec((rows, block), lambda i, core: (0, i)))
    return pl.pallas_call(
        turn_kernel,
        grid_spec=pltpu.PrefetchScalarGridSpec(
            num_scalar_prefetch=1,
            grid=(tokens // block,),
            in_specs=[
                pl.BlockSpec((block, half), lambda i, core: (i, core[0])),
                pl.BlockSpec((block, half), lambda i, core: (i, 1 - core[0])),
            ],
            out_specs=specs,
        ),
        out_shape=shapes,
        cost_estimate=pl.CostEstimate(flops=0, bytes_accessed=4 * tokens * width, transcendentals=0),
        compiler_params=pltpu.CompilerParams(vmem_limit_bytes=60 * 1024 * 1024),
        name="turn",
    )(core, activations, activations)


def product_kernel(count_a, count_b, origin, *refs):
    sources, queries, outs = refs[0:8], refs[8:12], refs[13:18]
    left, right, total, plus, minus, late_p, late_m, mine, left_sem, right_sem, out_sem = refs[18:]
    rows = sources[0].shape[0]
    tokens, cols = queries[0].shape
    blocks = tokens // TOKEN_BLOCK

    def left_copy(half, k):
        target = left.at[half, pl.ds(k * rows, rows)]
        return pltpu.make_async_copy(sources[half * NZ + k], target, left_sem.at[half, k])

    def right_copy(half, side, j):
        at = pl.ds(j * TOKEN_BLOCK, TOKEN_BLOCK)
        source = queries[half * 2 + side].at[at]
        target = right.at[half, at, pl.ds(side * cols, cols)]
        return pltpu.make_async_copy(source, target, right_sem.at[half, side, j])

    for half in range(2):
        for k in range(NZ):
            left_copy(half, k).start()
        for j in range(blocks):
            for side in range(2):
                right_copy(half, side, j).start()

    total[...] = jnp.zeros_like(total)

    def add(half, first_count, lo, size):
        at = pl.ds(pl.multiple_of(lo, size), size)
        e = jnp.where(first_count <= lo, 1, 0)
        total[e] += jnp.dot(left[half, :, at], right[half, at, :], preferred_element_type=jnp.float32)

    def is_mixed(first_count, lo, size):
        return jnp.logical_and(first_count > lo, first_count < lo + size)

    def chunk(t, carry):
        half, j = t // blocks, t % blocks
        first_count = jnp.where(half == 0, count_a[0], count_b[0])

        @pl.when(j == 0)
        def _():
            for k in range(NZ):
                target = left.at[half, pl.ds(k * rows, rows)]
                pltpu.make_async_copy(sources[k], target, left_sem.at[half, k]).wait()

        lo = pl.multiple_of(j * TOKEN_BLOCK, TOKEN_BLOCK)
        for side in range(2):
            target = right.at[half, pl.ds(lo, TOKEN_BLOCK), pl.ds(side * cols, cols)]
            source = queries[side].at[pl.ds(lo, TOKEN_BLOCK)]
            pltpu.make_async_copy(source, target, right_sem.at[half, side, j]).wait()
        mixed = is_mixed(first_count, lo, TOKEN_BLOCK)

        @pl.when(jnp.logical_not(mixed))
        def _():
            add(half, first_count, lo, TOKEN_BLOCK)

        @pl.when(mixed)
        def _():
            size = TOKEN_BLOCK // SPLIT

            def one(i, inner_carry):
                low = lo + i * size
                at = pl.ds(pl.multiple_of(low, size), size)
                query = right[half, at, :]
                is_first = lax.broadcasted_iota(jnp.int32, query.shape, 0) < first_count - low
                nothing = jnp.zeros_like(query)
                value = left[half, :, at]

                @pl.when(first_count > low)
                def _():
                    total[0] += jnp.dot(value, jnp.where(is_first, query, nothing), preferred_element_type=jnp.float32)

                @pl.when(first_count < low + size)
                def _():
                    total[1] += jnp.dot(value, jnp.where(is_first, nothing, query), preferred_element_type=jnp.float32)

                return inner_carry

            lax.fori_loop(0, SPLIT, one, 0)

        return carry

    lax.fori_loop(0, 2 * blocks, chunk, 0)

    def block(r, e):
        k = jnp.bitwise_and(origin[0] - r, NZ - 1)
        return total[e, pl.ds(pl.multiple_of(k * rows, rows), rows), :].astype(jnp.bfloat16)

    def out_copy(i):
        return pltpu.make_async_copy((plus, minus, late_p, late_m, mine)[i], outs[i], out_sem.at[i])

    plus[0] = block(2, 0)
    plus[1] = block(1, 1)
    out_copy(0).start()
    minus[0] = block(3, 0)
    minus[1] = block(2, 1)
    out_copy(1).start()
    late_p[...] = block(1, 0)
    out_copy(2).start()
    late_m[...] = block(3, 1)
    out_copy(3).start()
    mine[0] = block(0, 0)
    mine[1] = block(0, 1)
    out_copy(4).start()
    for i in range(5):
        out_copy(i).wait()


def product(info, left_a, left_b, q_a, qx_a, q_b, qx_b, after):
    rows, tokens = left_a[0].shape
    cols = q_a.shape[1]
    pair, single = (2, rows, 2 * cols), (rows, 2 * cols)
    shapes = [pair, pair, single, single, pair]
    smem = pl.BlockSpec(memory_space=pltpu.SMEM)
    anywhere = pl.BlockSpec(memory_space=pl.ANY)
    return pl.pallas_call(
        product_kernel,
        in_specs=[smem] * 3 + [anywhere] * 13,
        out_specs=[anywhere] * 5,
        out_shape=[jax.ShapeDtypeStruct(shape, jnp.bfloat16) for shape in shapes],
        scratch_shapes=[
            pltpu.VMEM((2, NZ * rows, tokens), jnp.bfloat16),
            pltpu.VMEM((2, tokens, 2 * cols), jnp.bfloat16),
            pltpu.VMEM((2, NZ * rows, 2 * cols), jnp.float32),
        ]
        + [pltpu.VMEM(shape, jnp.bfloat16) for shape in shapes]
        + [
            pltpu.SemaphoreType.DMA((2, NZ)),
            pltpu.SemaphoreType.DMA((2, 2, tokens // TOKEN_BLOCK)),
            pltpu.SemaphoreType.DMA((5,)),
        ],
        cost_estimate=pl.CostEstimate(
            flops=2 * 2 * tokens * NZ * rows * 2 * cols,
            bytes_accessed=2 * (2 * tokens * (NZ * rows + 2 * cols) + 8 * rows * 2 * cols),
            transcendentals=0,
        ),
        compiler_params=pltpu.CompilerParams(vmem_limit_bytes=60 * 1024 * 1024),
        name="product",
    )(*info, *left_a, *left_b, q_a, qx_a, q_b, qx_b, after)


def finish_kernel(
    info, squares, part_0, part_1, part_2, part_3, base, grads, flipped, ahead, momentum_new, update
):
    limit = clip_scale * math.sqrt(base.shape[1] * base.shape[1])
    sums = jnp.sum(squares[...], axis=0, keepdims=True)
    factors = limit / jnp.maximum(jnp.sqrt(sums), limit)
    cols = grads.shape[2]
    wide = [jnp.concatenate([factors[:, e * 128 : (e + 1) * 128]] * (cols // 128), axis=1) for e in range(2)]
    for k, part in enumerate((part_0, part_1, part_2, part_3)):
        origin = jnp.bitwise_and(info[0] - k, NZ - 1)
        for i, half in enumerate((info[1], 1 - info[1])):
            at = pl.ds(pl.multiple_of((origin * NXH + half) * cols, cols), cols)
            first = wide[0] * part[i, 0].astype(jnp.float32)
            second = wide[1] * part[i, 1].astype(jnp.float32)
            momentum_new[:, at] = base[:, at] + first + second

    def write(first, second):
        clipped = wide[0] * first + wide[1] * second
        total = (1.0 + momentum_decay) * clipped + ahead[...].astype(jnp.float32)
        update[...] = (-total).astype(jnp.bfloat16)

    @pl.when(info[2] == 1)
    def _():
        write(grads[0], grads[1])

    @pl.when(info[2] == 0)
    def _():
        write(flipped[0].astype(jnp.float32), flipped[1].astype(jnp.float32))


def finish(info, squares, parts, base, grads, flipped, ahead):
    return pl.pallas_call(
        finish_kernel,
        in_specs=[pl.BlockSpec(memory_space=pltpu.SMEM)] + [pl.BlockSpec(memory_space=pltpu.VMEM)] * 9,
        out_specs=[pl.BlockSpec(memory_space=pltpu.VMEM)] * 2,
        out_shape=[
            jax.ShapeDtypeStruct(base.shape, jnp.float32),
            jax.ShapeDtypeStruct(ahead.shape, jnp.bfloat16),
        ],
        compiler_params=pltpu.CompilerParams(vmem_limit_bytes=16 * 1024 * 1024),
        name="finish",
    )(info, squares, *parts, base, grads, flipped, ahead)


def step(activations, query_grad, example_ids, band_coefs, noise_history, momentum):
    f32, bf16 = jnp.float32, jnp.bfloat16
    ctx, head = lax.axis_index("ctx"), lax.axis_index("head")
    y, xl, core = ctx >> 2, (ctx >> 1) & 1, ctx & 1
    z, xh = head >> 1, head & 1
    head_cols = query_grad.shape[1]

    first_count = jnp.sum((example_ids == 0).astype(jnp.int32)).reshape(1)
    other_count = swap_core(first_count)
    info = (first_count, other_count, (z - y + NZ).reshape(1).astype(jnp.int32))

    pieces = turn(core.reshape(1).astype(jnp.int32), activations)

    qx = swap_xh(query_grad)
    q_other = swap_core(query_grad)
    qx_other = swap_core(qx)

    noise = jnp.sum(band_coefs.astype(f32)[:, None, None] * noise_history.astype(f32), axis=0)
    base = momentum_decay * momentum + noise_weight * noise
    ahead = ((1.0 + momentum_decay) * noise_weight * noise + momentum_decay**2 * momentum).astype(bf16)
    owner_rows = ahead.shape[0]
    ahead = ahead.reshape(owner_rows, NZ * NXH, head_cols).transpose(1, 0, 2)
    ahead = lax.all_to_all(ahead, "head", split_axis=0, concat_axis=0, tiled=True)
    ahead = ahead.reshape(-1, head_cols)

    same = xl == xh
    done = []
    for i in range(len(CHUNKS)):
        own = pieces[2 * i]
        taken = swap_core(pieces[2 * i + 1])
        up_own = shift_z(own, 1)
        up_taken = shift_z(taken, 1)
        down_taken = shift_z(taken, -1)
        down_own = shift_z(own, -1)
        far_own = shift_z(up_own, 1)
        far_taken = shift_z(down_taken, -1)
        plus, minus, late_p, late_m, mine = product(
            info,
            (own, up_own, far_own, down_own),
            (taken, up_taken, far_taken, down_taken),
            query_grad,
            qx,
            q_other,
            qx_other,
            ahead,
        )
        from_below = shift_y(plus, 1)
        from_above = shift_y(minus, -1)
        late_p = (late_p.astype(f32) + from_below[0].astype(f32)).astype(bf16)
        late_m = (late_m.astype(f32) + from_above[1].astype(f32)).astype(bf16)
        got_p = shift_y(late_p, 1)
        got_m = shift_y(late_m, -1)
        sum_first = mine[0].astype(f32) + got_p.astype(f32) + from_above[0].astype(f32)
        sum_second = mine[1].astype(f32) + from_below[1].astype(f32) + got_m.astype(f32)
        near = jnp.stack([sum_first[:, :head_cols], sum_second[:, :head_cols]])
        other = jnp.stack([sum_first[:, head_cols:], sum_second[:, head_cols:]])
        got = swap_xl(jnp.where(same, other, near).astype(bf16))
        total = got.astype(f32) + jnp.where(same, near, other)
        done.append(total)

    grads = jnp.concatenate(done, axis=1)
    squares = sum(jnp.sum(d * d, axis=(1, 2)) for d in done)
    count = lax.axis_size("ctx") * lax.axis_size("head")
    lanes = jnp.repeat(squares, 128)[None, :]
    all_squares = lax.all_to_all(jnp.broadcast_to(lanes, (count, 256)), BOTH, 0, 0, tiled=True)

    narrow = grads.astype(bf16)
    blocks = narrow.reshape(2, NZ, NXH, owner_rows, head_cols)
    far = gather_x(jnp.where(xl == 0, blocks[:, :, 1], blocks[:, :, 0]))
    near = jnp.where(xl == 0, blocks[:, :, 0], blocks[:, :, 1])
    near = jnp.where(same, near, cross_x(near))
    flipped = cross_x(narrow)
    both = jnp.stack([near, far])
    parts = [lax.dynamic_index_in_dim(both, z, 2, False)]
    for k in range(1, NZ):
        parts.append(shift_z(lax.dynamic_index_in_dim(both, (z + k) & (NZ - 1), 2, False), k))
    facts = jnp.stack([z, xh, same.astype(z.dtype)]).astype(jnp.int32)
    return finish(facts, all_squares, parts, base, grads, flipped, ahead)


def solution(mesh):
    in_specs = (
        P("ctx", "head"),
        P("ctx", "head"),
        P("ctx"),
        P(),
        P(None, ("ctx", "head"), None),
        P(("ctx", "head"), None),
    )
    out_specs = (P(("ctx", "head"), None), P("ctx", "head"))
    return jax.shard_map(step, mesh=mesh, in_specs=in_specs, out_specs=out_specs, check_vma=False)
```

profile of v0, /device:TPU:0, one launch (start us, length us, event | category | flops | bytes accessed | tf_op | source)
XLA Modules:
  0.0 190.9 jit_solution(9799331653433110982)
XLA Ops:
  0.6 3.2 %collective-permute-start.8 = (bf16[2048,512]{1,0:T(8,128)(2,1)}, bf16[2048,512]{1,0:T(8,128)(2,1)S(1)}, u32[]{:S(2)}, u32[]{:S(2)}) collective-permute-start(bf16[2048,512]{1,0:T(8,128)(2,1)} %refs_8_.3), channel_id=1, source_target_pairs={{0,1},{1,0},{2,3},{3,2},{4,5},{5,4},{6,7},{7,6},{8,9},{9,8},{10,11... | collective-permute-start | bytes 6291464 | tf_op jit(solution)/shard_map/ppermute | solution.py:34
  3.9 2.8 %turn.1 = (bf16[160,2048]{1,0:T(8,128)(2,1)}, bf16[160,2048]{1,0:T(8,128)(2,1)}, bf16[96,2048]{1,0:T(8,128)(2,1)}, bf16[96,2048]{1,0:T(8,128)(2,1)}) custom-call(s32[1]{0:T(128)} %bitcast.5.core, bf16[2048,512]{1,0:T(8,128)(2,1)} %give.1, bf16[2048,512]{1,0:T(8,128)(2,1)} %give.1), custom_call_target="tpu_custom_call" | custom-call | bytes 4194304 | tf_op jit(solution)/shard_map/turn/pallas_call | solution.py:91
  6.6 2.0 %collective-permute-start.16 = (bf16[96,2048]{1,0:T(8,128)(2,1)}, bf16[96,2048]{1,0:T(8,128)(2,1)S(1)}, u32[]{:S(2)}, u32[]{:S(2)}) collective-permute-start(bf16[96,2048]{1,0:T(8,128)(2,1)} %get-tuple-element.23.refs_0_), channel_id=1, source_target_pairs={{0,2},{1,3},{2,4},{3,5},{4,6},{5,7},{6,0},{7,1},{8,10},{9,11},{10,... | collective-permute-start | bytes 1179656 | tf_op jit(solution)/shard_map/ppermute | solution.py:34
  11.8 2.2 %collective-permute-start.18 = (bf16[96,2048]{1,0:T(8,128)(2,1)}, bf16[96,2048]{1,0:T(8,128)(2,1)S(1)}, u32[]{:S(2)}, u32[]{:S(2)}) collective-permute-start(bf16[96,2048]{1,0:T(8,128)(2,1)} %get-tuple-element.23.refs_0_), channel_id=1, source_target_pairs={{0,6},{1,7},{2,0},{3,1},{4,2},{5,3},{6,4},{7,5},{8,14},{9,15},{10,... | collective-permute-start | bytes 1179656 | tf_op jit(solution)/shard_map/ppermute | solution.py:34
  14.0 6.6 %collective-permute-done.16.refs_1_ = bf16[96,2048]{1,0:T(8,128)(2,1)S(1)} collective-permute-done((bf16[96,2048]{1,0:T(8,128)(2,1)}, bf16[96,2048]{1,0:T(8,128)(2,1)S(1)}, u32[]{:S(2)}, u32[]{:S(2)}) %collective-permute-start.16) | collective-permute-done | bytes 393248 | tf_op jit(solution)/shard_map/ppermute | solution.py:34
  20.6 2.7 %collective-permute-done.18.refs_3_ = bf16[96,2048]{1,0:T(8,128)(2,1)S(1)} collective-permute-done((bf16[96,2048]{1,0:T(8,128)(2,1)}, bf16[96,2048]{1,0:T(8,128)(2,1)S(1)}, u32[]{:S(2)}, u32[]{:S(2)}) %collective-permute-start.18) | collective-permute-done | bytes 393248 | tf_op jit(solution)/shard_map/ppermute | solution.py:34
  23.4 3.4 %collective-permute-start.21 = (bf16[96,2048]{1,0:T(8,128)(2,1)S(1)}, bf16[96,2048]{1,0:T(8,128)(2,1)S(1)}, u32[]{:S(2)}, u32[]{:S(2)}) collective-permute-start(bf16[96,2048]{1,0:T(8,128)(2,1)S(1)} %collective-permute-done.19.refs_4_), channel_id=1, source_target_pairs={{0,6},{1,7},{2,0},{3,1},{4,2},{5,3},{6,4},{7,5},{8,14},{9,15},{10,... | collective-permute-start | bytes 1179656 | tf_op jit(solution)/shard_map/ppermute | solution.py:34
  27.5 12.3 %collective-permute-done.1.refs_1_ = bf16[160,2048]{1,0:T(8,128)(2,1)} collective-permute-done((bf16[160,2048]{1,0:T(8,128)(2,1)}, bf16[160,2048]{1,0:T(8,128)(2,1)}, u32[]{:S(2)}, u32[]{:S(2)}) %collective-permute-start.1) | collective-permute-done | bytes 655392 | tf_op jit(solution)/shard_map/ppermute | solution.py:34
  39.8 3.2 %collective-permute-start.6 = (bf16[160,2048]{1,0:T(8,128)(2,1)}, bf16[160,2048]{1,0:T(8,128)(2,1)}, u32[]{:S(2)}, u32[]{:S(2)}) collective-permute-start(bf16[160,2048]{1,0:T(8,128)(2,1)} %collective-permute-done.4.refs_4_), channel_id=1, source_target_pairs={{0,6},{1,7},{2,0},{3,1},{4,2},{5,3},{6,4},{7,5},{8,14},{9,15},{10,... | collective-permute-start | bytes 1966088 | tf_op jit(solution)/shard_map/ppermute | solution.py:34
  43.0 5.1 %collective-permute-done.17.refs_2_ = bf16[96,2048]{1,0:T(8,128)(2,1)S(1)} collective-permute-done((bf16[96,2048]{1,0:T(8,128)(2,1)S(1)}, bf16[96,2048]{1,0:T(8,128)(2,1)S(1)}, u32[]{:S(2)}, u32[]{:S(2)}) %collective-permute-start.17) | collective-permute-done | bytes 393248 | tf_op jit(solution)/shard_map/ppermute | solution.py:34
  49.8 7.9 %multiply_reduce_fusion = f32[32,4096]{1,0:T(8,128)S(1)} fusion(bf16[64,32,4096]{2,1,0:T(8,128)(2,1)} %param.10, f32[64]{0:T(128)S(1)} %convert_element_type.133), kind=kLoop, calls=%fused_computation | loop fusion | flops 25034752 | bytes 17301760 | tf_op jit(solution)/shard_map/reduce_sum | solution.py:310
  57.8 4.3 %collective-permute-start.3 = (bf16[160,2048]{1,0:T(8,128)(2,1)}, bf16[160,2048]{1,0:T(8,128)(2,1)}, u32[]{:S(2)}, u32[]{:S(2)}) collective-permute-start(bf16[160,2048]{1,0:T(8,128)(2,1)} %get-tuple-element.16.refs_0_), channel_id=1, source_target_pairs={{0,6},{1,7},{2,0},{3,1},{4,2},{5,3},{6,4},{7,5},{8,14},{9,15},{10,... | collective-permute-start | bytes 1966088 | tf_op jit(solution)/shard_map/ppermute | solution.py:34
  62.1 3.1 %collective-permute-done.22.refs_6_ = bf16[96,2048]{1,0:T(8,128)(2,1)S(1)} collective-permute-done((bf16[96,2048]{1,0:T(8,128)(2,1)S(1)}, bf16[96,2048]{1,0:T(8,128)(2,1)S(1)}, u32[]{:S(2)}, u32[]{:S(2)}) %collective-permute-start.22) | collective-permute-done | bytes 393248 | tf_op jit(solution)/shard_map/ppermute | solution.py:34
  66.6 1.9 %collective-permute-start.7 = (bf16[160,2048]{1,0:T(8,128)(2,1)}, bf16[160,2048]{1,0:T(8,128)(2,1)}, u32[]{:S(2)}, u32[]{:S(2)}) collective-permute-start(bf16[160,2048]{1,0:T(8,128)(2,1)} %collective-permute-done.6.refs_7_), channel_id=1, source_target_pairs={{0,6},{1,7},{2,0},{3,1},{4,2},{5,3},{6,4},{7,5},{8,14},{9,15},{10,... | collective-permute-start | bytes 1966088 | tf_op jit(solution)/shard_map/ppermute | solution.py:34
  69.4 4.6 %all-to-all-start = ((bf16[8,32,512]{2,1,0:T(8,128)(2,1)}), bf16[8,32,512]{2,1,0:T(8,128)(2,1)S(1)}, u32[]{:S(2)}, u32[]{:S(2)}) async-start(bf16[8,32,512]{2,1,0:T(8,128)(2,1)} %bitcast.107), calls=%async_computation | async-start | bytes 524288 | tf_op jit(solution)/shard_map/all_to_all | solution.py:315
  74.0 23.0 %all-to-all-done = bf16[8,32,512]{2,1,0:T(8,128)(2,1)S(1)} async-done(((bf16[8,32,512]{2,1,0:T(8,128)(2,1)}), bf16[8,32,512]{2,1,0:T(8,128)(2,1)S(1)}, u32[]{:S(2)}, u32[]{:S(2)}) %all-to-all-start) | async-done | bytes 262176 | tf_op jit(solution)/shard_map/all_to_all | solution.py:315
  97.7 8.9 %product.3 = (bf16[2,96,1024]{2,1,0:T(8,128)(2,1)}, bf16[2,96,1024]{2,1,0:T(8,128)(2,1)}, bf16[96,1024]{1,0:T(8,128)(2,1)}, bf16[96,1024]{1,0:T(8,128)(2,1)}, bf16[2,96,1024]{2,1,0:T(8,128)(2,1)}) custom-call(s32[1]{0:T(128)} %bitcast.3.count_a, s32[1]{0:T(128)} %collective-permute-done.count_b, s32[1]{0:T(128)} %bitcast.4.origin, ...), custom_call_target="tpu_custom_call" | custom-call | flops 3221225472 | bytes 13107200 | tf_op jit(solution)/shard_map/product/pallas_call | solution.py:223
  106.7 3.1 %collective-permute-start.25 = (bf16[2,96,1024]{2,1,0:T(8,128)(2,1)}, bf16[2,96,1024]{2,1,0:T(8,128)(2,1)S(1)}, u32[]{:S(2)}, u32[]{:S(2)}) collective-permute-start(bf16[2,96,1024]{2,1,0:T(8,128)(2,1)} %get-tuple-element.28), channel_id=1, source_target_pairs={{0,96},{1,97},{2,98},{3,99},{4,100},{5,101},{6,102},{7,103},{8,104... | collective-permute-start | bytes 1179656 | tf_op jit(solution)/shard_map/ppermute | solution.py:34
  109.8 11.8 %product.2 = (bf16[2,160,1024]{2,1,0:T(8,128)(2,1)}, bf16[2,160,1024]{2,1,0:T(8,128)(2,1)}, bf16[160,1024]{1,0:T(8,128)(2,1)}, bf16[160,1024]{1,0:T(8,128)(2,1)}, bf16[2,160,1024]{2,1,0:T(8,128)(2,1)}) custom-call(s32[1]{0:T(128)} %bitcast.3.count_a, s32[1]{0:T(128)} %collective-permute-done.count_b, s32[1]{0:T(128)} %bitcast.4.origin, ...), custom_call_target="tpu_custom_call" | custom-call | flops 5368709120 | bytes 16252928 | tf_op jit(solution)/shard_map/product/pallas_call | solution.py:223
  121.6 3.3 %collective-permute-start.13 = (bf16[2,160,1024]{2,1,0:T(8,128)(2,1)}, bf16[2,160,1024]{2,1,0:T(8,128)(2,1)S(1)}, u32[]{:S(2)}, u32[]{:S(2)}) collective-permute-start(bf16[2,160,1024]{2,1,0:T(8,128)(2,1)} %get-tuple-element.21), channel_id=1, source_target_pairs={{0,96},{1,97},{2,98},{3,99},{4,100},{5,101},{6,102},{7,103},{8,104... | collective-permute-start | bytes 1966088 | tf_op jit(solution)/shard_map/ppermute | solution.py:34
  125.9 2.0 %collective-permute-start.24 = (bf16[96,1024]{1,0:T(8,128)(2,1)}, bf16[96,1024]{1,0:T(8,128)(2,1)}, u32[]{:S(2)}, u32[]{:S(2)}) collective-permute-start(bf16[96,1024]{1,0:T(8,128)(2,1)} %fusion.3), channel_id=1, source_target_pairs={{0,32},{1,33},{2,34},{3,35},{4,36},{5,37},{6,38},{7,39},{8,40},{9,... | collective-permute-start | bytes 589832 | tf_op jit(solution)/shard_map/ppermute | solution.py:34
  127.9 11.0 %collective-permute-done.26 = bf16[96,1024]{1,0:T(8,128)(2,1)} collective-permute-done((bf16[96,1024]{1,0:T(8,128)(2,1)S(1)}, bf16[96,1024]{1,0:T(8,128)(2,1)}, u32[]{:S(2)}, u32[]{:S(2)}) %collective-permute-start.26) | collective-permute-done | bytes 196640 | tf_op jit(solution)/shard_map/ppermute | solution.py:34
  141.2 3.9 %collective-permute-start.14 = (bf16[160,1024]{1,0:T(8,128)(2,1)S(1)}, bf16[160,1024]{1,0:T(8,128)(2,1)S(1)}, u32[]{:S(2)}, u32[]{:S(2)}) collective-permute-start(bf16[160,1024]{1,0:T(8,128)(2,1)S(1)} %fusion), channel_id=1, source_target_pairs={{0,96},{1,97},{2,98},{3,99},{4,100},{5,101},{6,102},{7,103},{8,104... | collective-permute-start | bytes 983048 | tf_op jit(solution)/shard_map/ppermute | solution.py:34
  146.4 2.4 %collective-permute-start.27 = (bf16[2,96,512]{2,1,0:T(8,128)(2,1)S(1)}, bf16[2,96,512]{2,1,0:T(8,128)(2,1)S(1)}, u32[]{:S(2)}, u32[]{:S(2)}) collective-permute-start(bf16[2,96,512]{2,1,0:T(8,128)(2,1)S(1)} %select_convert_fusion.1), channel_id=1, source_target_pairs={{0,16},{1,17},{2,18},{3,19},{4,20},{5,21},{6,22},{7,23},{8,24},{9,... | collective-permute-start | bytes 589832 | tf_op jit(solution)/shard_map/ppermute | solution.py:34
  149.7 4.8 %collective-permute-done.12 = bf16[160,1024]{1,0:T(8,128)(2,1)S(1)} collective-permute-done((bf16[160,1024]{1,0:T(8,128)(2,1)S(1)}, bf16[160,1024]{1,0:T(8,128)(2,1)S(1)}, u32[]{:S(2)}, u32[]{:S(2)}) %collective-permute-start.12) | collective-permute-done | bytes 327712 | tf_op jit(solution)/shard_map/ppermute | solution.py:34
  156.1 2.4 %collective-permute-start.15 = (bf16[2,160,512]{2,1,0:T(8,128)(2,1)S(1)}, bf16[2,160,512]{2,1,0:T(8,128)(2,1)S(1)}, u32[]{:S(2)}, u32[]{:S(2)}) collective-permute-start(bf16[2,160,512]{2,1,0:T(8,128)(2,1)S(1)} %select_convert_fusion), channel_id=1, source_target_pairs={{0,16},{1,17},{2,18},{3,19},{4,20},{5,21},{6,22},{7,23},{8,24},{9,... | collective-permute-start | bytes 983048 | tf_op jit(solution)/shard_map/ppermute | solution.py:34
  158.8 4.8 %collective-permute-done.15 = bf16[2,160,512]{2,1,0:T(8,128)(2,1)S(1)} collective-permute-done((bf16[2,160,512]{2,1,0:T(8,128)(2,1)S(1)}, bf16[2,160,512]{2,1,0:T(8,128)(2,1)S(1)}, u32[]{:S(2)}, u32[]{:S(2)}) %collective-permute-start.15) | collective-permute-done | bytes 327712 | tf_op jit(solution)/shard_map/ppermute | solution.py:34
  164.0 4.4 %collective-permute-start.28 = (bf16[2,4,32,512]{3,2,1,0:T(8,128)(2,1)S(1)}, bf16[2,4,32,512]{3,2,1,0:T(8,128)(2,1)S(1)}, u32[]{:S(2)}, u32[]{:S(2)}) collective-permute-start(bf16[2,4,32,512]{3,2,1,0:T(8,128)(2,1)S(1)} %fusion.5), channel_id=1, source_target_pairs={{0,17},{1,16},{2,19},{3,18},{4,21},{5,20},{6,23},{7,22},{8,25},{9,... | collective-permute-start | bytes 786440 | tf_op jit(solution)/shard_map/ppermute | solution.py:34
  169.2 1.8 collective-permute-start.29
  171.8 4.7 %all-to-all-start.1 = ((f32[128,1,256]{2,1,0:T(1,128)}), f32[128,1,256]{2,1,0:T(1,128)S(1)}, u32[]{:S(2)}, u32[]{:S(2)}) async-start(f32[128,1,256]{2,1,0:T(1,128)} %broadcast_in_dim.13), calls=%async_computation.1 | async-start | bytes 262144 | tf_op jit(solution)/shard_map/all_to_all | solution.py:357
  178.5 3.2 %collective-permute-start.31 = (bf16[2,2,32,512]{3,2,1,0:T(8,128)(2,1)}, bf16[2,2,32,512]{3,2,1,0:T(8,128)(2,1)S(1)}, u32[]{:S(2)}, u32[]{:S(2)}) collective-permute-start(bf16[2,2,32,512]{3,2,1,0:T(8,128)(2,1)} %get-tuple-element.45), channel_id=1, source_target_pairs={{0,4},{1,5},{2,6},{3,7},{4,0},{5,1},{6,2},{7,3},{8,12},{9,13},{10,... | collective-permute-start | bytes 393224 | tf_op jit(solution)/shard_map/ppermute | solution.py:34
  185.8 3.4 %collective-permute-done.31.part_2 = bf16[2,2,32,512]{3,2,1,0:T(8,128)(2,1)S(1)} collective-permute-done((bf16[2,2,32,512]{3,2,1,0:T(8,128)(2,1)}, bf16[2,2,32,512]{3,2,1,0:T(8,128)(2,1)S(1)}, u32[]{:S(2)}, u32[]{:S(2)}) %collective-permute-start.31) | collective-permute-done | bytes 131104 | tf_op jit(solution)/shard_map/ppermute | solution.py:34
  (106 shorter events, 25.5 us)
Async XLA Ops:
  0.6 49.1 %collective-permute-start.8 = (bf16[2048,512]{1,0:T(8,128)(2,1)}, bf16[2048,512]{1,0:T(8,128)(2,1)S(1)}, u32[]{:S(2)}, u32[]{:S(2)}) collective-permute-start(bf16[2048,512]{1,0:T(8,128)(2,1)} %refs_8_.3), channel_id=1, source_target_pairs={{0,1},{1,0},{2,3},{3,2},{4,5},{5,4},{6,7},{7,6},{8,9},{9,8},{10,11... | collective-permute-start | bytes 6291464 | tf_op jit(solution)/shard_map/ppermute | solution.py:34
  6.6 14.0 %collective-permute-start.16 = (bf16[96,2048]{1,0:T(8,128)(2,1)}, bf16[96,2048]{1,0:T(8,128)(2,1)S(1)}, u32[]{:S(2)}, u32[]{:S(2)}) collective-permute-start(bf16[96,2048]{1,0:T(8,128)(2,1)} %get-tuple-element.23.refs_0_), channel_id=1, source_target_pairs={{0,2},{1,3},{2,4},{3,5},{4,6},{5,7},{6,0},{7,1},{8,10},{9,11},{10,... | collective-permute-start | bytes 1179656 | tf_op jit(solution)/shard_map/ppermute | solution.py:34
  8.6 18.2 %collective-permute-start.4 = (bf16[160,2048]{1,0:T(8,128)(2,1)}, bf16[160,2048]{1,0:T(8,128)(2,1)}, u32[]{:S(2)}, u32[]{:S(2)}) collective-permute-start(bf16[160,2048]{1,0:T(8,128)(2,1)} %get-tuple-element.17), channel_id=1, source_target_pairs={{0,8},{1,9},{2,10},{3,11},{4,12},{5,13},{6,14},{7,15},{8,0},{9,1},... | collective-permute-start | bytes 1966088 | tf_op jit(solution)/shard_map/ppermute | solution.py:34
  11.5 55.2 %collective-permute-start.9 = (bf16[2048,512]{1,0:T(8,128)(2,1)}, bf16[2048,512]{1,0:T(8,128)(2,1)S(1)}, u32[]{:S(2)}, u32[]{:S(2)}) collective-permute-start(bf16[2048,512]{1,0:T(8,128)(2,1)} %refs_8_.3), channel_id=1, source_target_pairs={{0,8},{1,9},{2,10},{3,11},{4,12},{5,13},{6,14},{7,15},{8,0},{9,1},... | collective-permute-start | bytes 6291464 | tf_op jit(solution)/shard_map/ppermute | solution.py:34
  11.8 11.6 %collective-permute-start.18 = (bf16[96,2048]{1,0:T(8,128)(2,1)}, bf16[96,2048]{1,0:T(8,128)(2,1)S(1)}, u32[]{:S(2)}, u32[]{:S(2)}) collective-permute-start(bf16[96,2048]{1,0:T(8,128)(2,1)} %get-tuple-element.23.refs_0_), channel_id=1, source_target_pairs={{0,6},{1,7},{2,0},{3,1},{4,2},{5,3},{6,4},{7,5},{8,14},{9,15},{10,... | collective-permute-start | bytes 1179656 | tf_op jit(solution)/shard_map/ppermute | solution.py:34
  20.6 19.1 %collective-permute-start.1 = (bf16[160,2048]{1,0:T(8,128)(2,1)}, bf16[160,2048]{1,0:T(8,128)(2,1)}, u32[]{:S(2)}, u32[]{:S(2)}) collective-permute-start(bf16[160,2048]{1,0:T(8,128)(2,1)} %get-tuple-element.16.refs_0_), channel_id=1, source_target_pairs={{0,2},{1,3},{2,4},{3,5},{4,6},{5,7},{6,0},{7,1},{8,10},{9,11},{10,... | collective-permute-start | bytes 1966088 | tf_op jit(solution)/shard_map/ppermute | solution.py:34
  23.4 16.4 %collective-permute-start.21 = (bf16[96,2048]{1,0:T(8,128)(2,1)S(1)}, bf16[96,2048]{1,0:T(8,128)(2,1)S(1)}, u32[]{:S(2)}, u32[]{:S(2)}) collective-permute-start(bf16[96,2048]{1,0:T(8,128)(2,1)S(1)} %collective-permute-done.19.refs_4_), channel_id=1, source_target_pairs={{0,6},{1,7},{2,0},{3,1},{4,2},{5,3},{6,4},{7,5},{8,14},{9,15},{10,... | collective-permute-start | bytes 1179656 | tf_op jit(solution)/shard_map/ppermute | solution.py:34
  26.8 21.3 %collective-permute-start.17 = (bf16[96,2048]{1,0:T(8,128)(2,1)S(1)}, bf16[96,2048]{1,0:T(8,128)(2,1)S(1)}, u32[]{:S(2)}, u32[]{:S(2)}) collective-permute-start(bf16[96,2048]{1,0:T(8,128)(2,1)S(1)} %collective-permute-done.16.refs_1_), channel_id=1, source_target_pairs={{0,2},{1,3},{2,4},{3,5},{4,6},{5,7},{6,0},{7,1},{8,10},{9,11},{10,... | collective-permute-start | bytes 1179656 | tf_op jit(solution)/shard_map/ppermute | solution.py:34
  39.8 18.0 %collective-permute-start.20 = (bf16[96,2048]{1,0:T(8,128)(2,1)S(1)}, bf16[96,2048]{1,0:T(8,128)(2,1)S(1)}, u32[]{:S(2)}, u32[]{:S(2)}) collective-permute-start(bf16[96,2048]{1,0:T(8,128)(2,1)S(1)} %collective-permute-done.19.refs_4_), channel_id=1, source_target_pairs={{0,2},{1,3},{2,4},{3,5},{4,6},{5,7},{6,0},{7,1},{8,10},{9,11},{10,... | collective-permute-start | bytes 1179656 | tf_op jit(solution)/shard_map/ppermute | solution.py:34
  39.8 25.4 %collective-permute-start.6 = (bf16[160,2048]{1,0:T(8,128)(2,1)}, bf16[160,2048]{1,0:T(8,128)(2,1)}, u32[]{:S(2)}, u32[]{:S(2)}) collective-permute-start(bf16[160,2048]{1,0:T(8,128)(2,1)} %collective-permute-done.4.refs_4_), channel_id=1, source_target_pairs={{0,6},{1,7},{2,0},{3,1},{4,2},{5,3},{6,4},{7,5},{8,14},{9,15},{10,... | collective-permute-start | bytes 1966088 | tf_op jit(solution)/shard_map/ppermute | solution.py:34
  48.1 17.1 %collective-permute-start.22 = (bf16[96,2048]{1,0:T(8,128)(2,1)S(1)}, bf16[96,2048]{1,0:T(8,128)(2,1)S(1)}, u32[]{:S(2)}, u32[]{:S(2)}) collective-permute-start(bf16[96,2048]{1,0:T(8,128)(2,1)S(1)} %collective-permute-done.21.refs_7_), channel_id=1, source_target_pairs={{0,6},{1,7},{2,0},{3,1},{4,2},{5,3},{6,4},{7,5},{8,14},{9,15},{10,... | collective-permute-start | bytes 1179656 | tf_op jit(solution)/shard_map/ppermute | solution.py:34
  49.7 47.3 %collective-permute-start.10 = (bf16[2048,512]{1,0:T(8,128)(2,1)S(1)}, bf16[2048,512]{1,0:T(8,128)(2,1)}, u32[]{:S(2)}, u32[]{:S(2)}) collective-permute-start(bf16[2048,512]{1,0:T(8,128)(2,1)S(1)} %collective-permute-done.8.refs_9_), channel_id=1, source_target_pairs={{0,8},{1,9},{2,10},{3,11},{4,12},{5,13},{6,14},{7,15},{8,0},{9,1},... | collective-permute-start | bytes 6291464 | tf_op jit(solution)/shard_map/ppermute | solution.py:34
  57.8 52.0 %collective-permute-start.3 = (bf16[160,2048]{1,0:T(8,128)(2,1)}, bf16[160,2048]{1,0:T(8,128)(2,1)}, u32[]{:S(2)}, u32[]{:S(2)}) collective-permute-start(bf16[160,2048]{1,0:T(8,128)(2,1)} %get-tuple-element.16.refs_0_), channel_id=1, source_target_pairs={{0,6},{1,7},{2,0},{3,1},{4,2},{5,3},{6,4},{7,5},{8,14},{9,15},{10,... | collective-permute-start | bytes 1966088 | tf_op jit(solution)/shard_map/ppermute | solution.py:34
  65.2 44.7 %collective-permute-start.5 = (bf16[160,2048]{1,0:T(8,128)(2,1)}, bf16[160,2048]{1,0:T(8,128)(2,1)}, u32[]{:S(2)}, u32[]{:S(2)}) collective-permute-start(bf16[160,2048]{1,0:T(8,128)(2,1)} %collective-permute-done.4.refs_4_), channel_id=1, source_target_pairs={{0,2},{1,3},{2,4},{3,5},{4,6},{5,7},{6,0},{7,1},{8,10},{9,11},{10,... | collective-permute-start | bytes 1966088 | tf_op jit(solution)/shard_map/ppermute | solution.py:34
  65.2 44.6 %collective-permute-start.2 = (bf16[160,2048]{1,0:T(8,128)(2,1)}, bf16[160,2048]{1,0:T(8,128)(2,1)}, u32[]{:S(2)}, u32[]{:S(2)}) collective-permute-start(bf16[160,2048]{1,0:T(8,128)(2,1)} %collective-permute-done.1.refs_1_), channel_id=1, source_target_pairs={{0,2},{1,3},{2,4},{3,5},{4,6},{5,7},{6,0},{7,1},{8,10},{9,11},{10,... | collective-permute-start | bytes 1966088 | tf_op jit(solution)/shard_map/ppermute | solution.py:34
  66.6 43.2 %collective-permute-start.7 = (bf16[160,2048]{1,0:T(8,128)(2,1)}, bf16[160,2048]{1,0:T(8,128)(2,1)}, u32[]{:S(2)}, u32[]{:S(2)}) collective-permute-start(bf16[160,2048]{1,0:T(8,128)(2,1)} %collective-permute-done.6.refs_7_), channel_id=1, source_target_pairs={{0,6},{1,7},{2,0},{3,1},{4,2},{5,3},{6,4},{7,5},{8,14},{9,15},{10,... | collective-permute-start | bytes 1966088 | tf_op jit(solution)/shard_map/ppermute | solution.py:34
  69.4 27.6 %all-to-all-start = ((bf16[8,32,512]{2,1,0:T(8,128)(2,1)}), bf16[8,32,512]{2,1,0:T(8,128)(2,1)S(1)}, u32[]{:S(2)}, u32[]{:S(2)}) async-start(bf16[8,32,512]{2,1,0:T(8,128)(2,1)} %bitcast.107), calls=%async_computation | async-start | bytes 524288 | tf_op jit(solution)/shard_map/all_to_all | solution.py:315
  106.7 18.2 %collective-permute-start.25 = (bf16[2,96,1024]{2,1,0:T(8,128)(2,1)}, bf16[2,96,1024]{2,1,0:T(8,128)(2,1)S(1)}, u32[]{:S(2)}, u32[]{:S(2)}) collective-permute-start(bf16[2,96,1024]{2,1,0:T(8,128)(2,1)} %get-tuple-element.28), channel_id=1, source_target_pairs={{0,96},{1,97},{2,98},{3,99},{4,100},{5,101},{6,102},{7,103},{8,104... | collective-permute-start | bytes 1179656 | tf_op jit(solution)/shard_map/ppermute | solution.py:34
  109.8 15.3 %collective-permute-start.23 = (bf16[2,96,1024]{2,1,0:T(8,128)(2,1)}, bf16[2,96,1024]{2,1,0:T(8,128)(2,1)S(1)}, u32[]{:S(2)}, u32[]{:S(2)}) collective-permute-start(bf16[2,96,1024]{2,1,0:T(8,128)(2,1)} %get-tuple-element.27), channel_id=1, source_target_pairs={{0,32},{1,33},{2,34},{3,35},{4,36},{5,37},{6,38},{7,39},{8,40},{9,... | collective-permute-start | bytes 1179656 | tf_op jit(solution)/shard_map/ppermute | solution.py:34
  121.6 18.5 %collective-permute-start.13 = (bf16[2,160,1024]{2,1,0:T(8,128)(2,1)}, bf16[2,160,1024]{2,1,0:T(8,128)(2,1)S(1)}, u32[]{:S(2)}, u32[]{:S(2)}) collective-permute-start(bf16[2,160,1024]{2,1,0:T(8,128)(2,1)} %get-tuple-element.21), channel_id=1, source_target_pairs={{0,96},{1,97},{2,98},{3,99},{4,100},{5,101},{6,102},{7,103},{8,104... | collective-permute-start | bytes 1966088 | tf_op jit(solution)/shard_map/ppermute | solution.py:34
  125.0 13.9 %collective-permute-start.26 = (bf16[96,1024]{1,0:T(8,128)(2,1)S(1)}, bf16[96,1024]{1,0:T(8,128)(2,1)}, u32[]{:S(2)}, u32[]{:S(2)}) collective-permute-start(bf16[96,1024]{1,0:T(8,128)(2,1)S(1)} %fusion.2), channel_id=1, source_target_pairs={{0,96},{1,97},{2,98},{3,99},{4,100},{5,101},{6,102},{7,103},{8,104... | collective-permute-start | bytes 589832 | tf_op jit(solution)/shard_map/ppermute | solution.py:34
  125.9 13.1 %collective-permute-start.24 = (bf16[96,1024]{1,0:T(8,128)(2,1)}, bf16[96,1024]{1,0:T(8,128)(2,1)}, u32[]{:S(2)}, u32[]{:S(2)}) collective-permute-start(bf16[96,1024]{1,0:T(8,128)(2,1)} %fusion.3), channel_id=1, source_target_pairs={{0,32},{1,33},{2,34},{3,35},{4,36},{5,37},{6,38},{7,39},{8,40},{9,... | collective-permute-start | bytes 589832 | tf_op jit(solution)/shard_map/ppermute | solution.py:34
  127.8 17.2 %collective-permute-start.11 = (bf16[2,160,1024]{2,1,0:T(8,128)(2,1)}, bf16[2,160,1024]{2,1,0:T(8,128)(2,1)S(1)}, u32[]{:S(2)}, u32[]{:S(2)}) collective-permute-start(bf16[2,160,1024]{2,1,0:T(8,128)(2,1)} %get-tuple-element.20), channel_id=1, source_target_pairs={{0,32},{1,33},{2,34},{3,35},{4,36},{5,37},{6,38},{7,39},{8,40},{9,... | collective-permute-start | bytes 1966088 | tf_op jit(solution)/shard_map/ppermute | solution.py:34
  141.2 8.5 %collective-permute-start.14 = (bf16[160,1024]{1,0:T(8,128)(2,1)S(1)}, bf16[160,1024]{1,0:T(8,128)(2,1)S(1)}, u32[]{:S(2)}, u32[]{:S(2)}) collective-permute-start(bf16[160,1024]{1,0:T(8,128)(2,1)S(1)} %fusion), channel_id=1, source_target_pairs={{0,96},{1,97},{2,98},{3,99},{4,100},{5,101},{6,102},{7,103},{8,104... | collective-permute-start | bytes 983048 | tf_op jit(solution)/shard_map/ppermute | solution.py:34
  146.2 8.4 %collective-permute-start.12 = (bf16[160,1024]{1,0:T(8,128)(2,1)S(1)}, bf16[160,1024]{1,0:T(8,128)(2,1)S(1)}, u32[]{:S(2)}, u32[]{:S(2)}) collective-permute-start(bf16[160,1024]{1,0:T(8,128)(2,1)S(1)} %fusion.1), channel_id=1, source_target_pairs={{0,32},{1,33},{2,34},{3,35},{4,36},{5,37},{6,38},{7,39},{8,40},{9,... | collective-permute-start | bytes 983048 | tf_op jit(solution)/shard_map/ppermute | solution.py:34
  146.4 12.2 %collective-permute-start.27 = (bf16[2,96,512]{2,1,0:T(8,128)(2,1)S(1)}, bf16[2,96,512]{2,1,0:T(8,128)(2,1)S(1)}, u32[]{:S(2)}, u32[]{:S(2)}) collective-permute-start(bf16[2,96,512]{2,1,0:T(8,128)(2,1)S(1)} %select_convert_fusion.1), channel_id=1, source_target_pairs={{0,16},{1,17},{2,18},{3,19},{4,20},{5,21},{6,22},{7,23},{8,24},{9,... | collective-permute-start | bytes 589832 | tf_op jit(solution)/shard_map/ppermute | solution.py:34
  164.0 12.5 %collective-permute-start.28 = (bf16[2,4,32,512]{3,2,1,0:T(8,128)(2,1)S(1)}, bf16[2,4,32,512]{3,2,1,0:T(8,128)(2,1)S(1)}, u32[]{:S(2)}, u32[]{:S(2)}) collective-permute-start(bf16[2,4,32,512]{3,2,1,0:T(8,128)(2,1)S(1)} %fusion.5), channel_id=1, source_target_pairs={{0,17},{1,16},{2,19},{3,18},{4,21},{5,20},{6,23},{7,22},{8,25},{9,... | collective-permute-start | bytes 786440 | tf_op jit(solution)/shard_map/ppermute | solution.py:34
  168.5 20.7 %collective-permute-start.33 = (bf16[2,256,512]{2,1,0:T(8,128)(2,1)S(1)}, bf16[2,256,512]{2,1,0:T(8,128)(2,1)S(1)}, u32[]{:S(2)}, u32[]{:S(2)}) collective-permute-start(bf16[2,256,512]{2,1,0:T(8,128)(2,1)S(1)} %fusion.14), channel_id=1, source_target_pairs={{0,17},{1,16},{2,19},{3,18},{4,21},{5,20},{6,23},{7,22},{8,25},{9,... | collective-permute-start | bytes 1572872 | tf_op jit(solution)/shard_map/ppermute | solution.py:34
  171.8 14.0 %all-to-all-start.1 = ((f32[128,1,256]{2,1,0:T(1,128)}), f32[128,1,256]{2,1,0:T(1,128)S(1)}, u32[]{:S(2)}, u32[]{:S(2)}) async-start(f32[128,1,256]{2,1,0:T(1,128)} %broadcast_in_dim.13), calls=%async_computation.1 | async-start | bytes 262144 | tf_op jit(solution)/shard_map/all_to_all | solution.py:357
  177.4 8.4 %collective-permute-start.30 = (bf16[2,2,32,512]{3,2,1,0:T(8,128)(2,1)}, bf16[2,2,32,512]{3,2,1,0:T(8,128)(2,1)S(1)}, u32[]{:S(2)}, u32[]{:S(2)}) collective-permute-start(bf16[2,2,32,512]{3,2,1,0:T(8,128)(2,1)} %get-tuple-element.44), channel_id=1, source_target_pairs={{0,2},{1,3},{2,4},{3,5},{4,6},{5,7},{6,0},{7,1},{8,10},{9,11},{10,... | collective-permute-start | bytes 393224 | tf_op jit(solution)/shard_map/ppermute | solution.py:34
  178.5 10.7 %collective-permute-start.31 = (bf16[2,2,32,512]{3,2,1,0:T(8,128)(2,1)}, bf16[2,2,32,512]{3,2,1,0:T(8,128)(2,1)S(1)}, u32[]{:S(2)}, u32[]{:S(2)}) collective-permute-start(bf16[2,2,32,512]{3,2,1,0:T(8,128)(2,1)} %get-tuple-element.45), channel_id=1, source_target_pairs={{0,4},{1,5},{2,6},{3,7},{4,0},{5,1},{6,2},{7,3},{8,12},{9,13},{10,... | collective-permute-start | bytes 393224 | tf_op jit(solution)/shard_map/ppermute | solution.py:34
  181.7 7.5 %collective-permute-start.32 = (bf16[2,2,32,512]{3,2,1,0:T(8,128)(2,1)}, bf16[2,2,32,512]{3,2,1,0:T(8,128)(2,1)S(1)}, u32[]{:S(2)}, u32[]{:S(2)}) collective-permute-start(bf16[2,2,32,512]{3,2,1,0:T(8,128)(2,1)} %get-tuple-element.42), channel_id=1, source_target_pairs={{0,6},{1,7},{2,0},{3,1},{4,2},{5,3},{6,4},{7,5},{8,14},{9,15},{10,... | collective-permute-start | bytes 393224 | tf_op jit(solution)/shard_map/ppermute | solution.py:34
  (21 other events, 448.1 us)
where the time goes:
time: 192 us; the launch traced here: 191 us
  waiting for transfers between devices  81.5 us (42%)
  starting transfers between devices  62.2 us (32%)
  Pallas kernels  25.2 us (13%)
  other arithmetic  18.5 us (10%)
  local copies, waits for them, and re-layouts  2.46 us (1%)
    ppermute x34, waiting for transfers between devices, permute(): return lax.ppermute(value, BOTH, pairs)  56.9 us
    ppermute x34, starting transfers between devices, permute(): return lax.ppermute(value, BOTH, pairs)  53 us
    all_to_all x1, waiting for transfers between devices, step(): lax.all_to_all(ahead, 'head', split_axis=0, concat_axis=0, tiled=True)  23 us
    pallas_call x2, Pallas kernels, product(): pl.pallas_call(product_kernel, in_specs=[smem] * 3 + [anywhere] * 13, out...  20.7 us
    reduce_sum x1, other arithmetic, step(): jnp.sum(band_coefs.astype(f32)[:, None, None] * noise_history.astype(f32)...  7.92 us
    all_to_all x1, starting transfers between devices, step(): lax.all_to_all(jnp.broadcast_to(lanes, (count, 256)), BOTH, 0, 0, tiled=T...  4.67 us
    all_to_all x1, starting transfers between devices, step(): lax.all_to_all(ahead, 'head', split_axis=0, concat_axis=0, tiled=True)  4.58 us
  transfers between devices with their start and end apart: 36, of which 14 were waited for; matrix products, arithmetic and copies ran while one was open for 10% of the time, Pallas kernels for 12%

commit v1 on v0

--- a/solution.py
+++ b/solution.py
@@ -14,7 +14,7 @@
 
 BOTH = ("ctx", "head")
 NY, NXL, NCORE, NZ, NXH = 4, 2, 2, 4, 2
-CHUNKS = (160, 96)
+CHUNKS = (144, 112)
 TOKEN_BLOCK = 1024
 SPLIT = 2
 
@@ -107,8 +107,9 @@
 
 
 def product_kernel(count_a, count_b, origin, *refs):
-    sources, queries, outs = refs[0:8], refs[8:12], refs[13:18]
-    left, right, total, plus, minus, late_p, late_m, mine, left_sem, right_sem, out_sem = refs[18:]
+    sources, queries, outs = refs[0:8], refs[8:12], refs[13:20]
+    left, right, total = refs[20:23]
+    staged, (left_sem, right_sem, out_sem) = refs[23:30], refs[30:]
     rows = sources[0].shape[0]
     tokens, cols = queries[0].shape
     blocks = tokens // TOKEN_BLOCK
@@ -194,22 +195,15 @@
         return total[e, pl.ds(pl.multiple_of(k * rows, rows), rows), :].astype(jnp.bfloat16)
 
     def out_copy(i):
-        return pltpu.make_async_copy((plus, minus, late_p, late_m, mine)[i], outs[i], out_sem.at[i])
-
-    plus[0] = block(2, 0)
-    plus[1] = block(1, 1)
-    out_copy(0).start()
-    minus[0] = block(3, 0)
-    minus[1] = block(2, 1)
-    out_copy(1).start()
-    late_p[...] = block(1, 0)
-    out_copy(2).start()
-    late_m[...] = block(3, 1)
-    out_copy(3).start()
-    mine[0] = block(0, 0)
-    mine[1] = block(0, 1)
-    out_copy(4).start()
-    for i in range(5):
+        return pltpu.make_async_copy(staged[i], outs[i], out_sem.at[i])
+
+    for i, (r, e) in enumerate(((2, 0), (2, 1), (1, 1), (3, 0), (1, 0), (3, 1))):
+        staged[i][...] = block(r, e)
+        out_copy(i).start()
+    staged[6][0] = block(0, 0)
+    staged[6][1] = block(0, 1)
+    out_copy(6).start()
+    for i in range(7):
         out_copy(i).wait()
 
 
@@ -217,13 +211,13 @@
     rows, tokens = left_a[0].shape
     cols = q_a.shape[1]
     pair, single = (2, rows, 2 * cols), (rows, 2 * cols)
-    shapes = [pair, pair, single, single, pair]
+    shapes = [single] * 6 + [pair]
     smem = pl.BlockSpec(memory_space=pltpu.SMEM)
     anywhere = pl.BlockSpec(memory_space=pl.ANY)
     return pl.pallas_call(
         product_kernel,
         in_specs=[smem] * 3 + [anywhere] * 13,
-        out_specs=[anywhere] * 5,
+        out_specs=[anywhere] * 7,
         out_shape=[jax.ShapeDtypeStruct(shape, jnp.bfloat16) for shape in shapes],
         scratch_shapes=[
             pltpu.VMEM((2, NZ * rows, tokens), jnp.bfloat16),
@@ -234,14 +228,14 @@
         + [
             pltpu.SemaphoreType.DMA((2, NZ)),
             pltpu.SemaphoreType.DMA((2, 2, tokens // TOKEN_BLOCK)),
-            pltpu.SemaphoreType.DMA((5,)),
+            pltpu.SemaphoreType.DMA((7,)),
         ],
         cost_estimate=pl.CostEstimate(
             flops=2 * 2 * tokens * NZ * rows * 2 * cols,
             bytes_accessed=2 * (2 * tokens * (NZ * rows + 2 * cols) + 8 * rows * 2 * cols),
             transcendentals=0,
         ),
-        compiler_params=pltpu.CompilerParams(vmem_limit_bytes=60 * 1024 * 1024),
+        compiler_params=pltpu.CompilerParams(vmem_limit_bytes=28 * 1024 * 1024),
         name="product",
     )(*info, *left_a, *left_b, q_a, qx_a, q_b, qx_b, after)
 
@@ -326,7 +320,7 @@
         down_own = shift_z(own, -1)
         far_own = shift_z(up_own, 1)
         far_taken = shift_z(down_taken, -1)
-        plus, minus, late_p, late_m, mine = product(
+        far_p, far_m, near_p, near_m, late_p, late_m, mine = product(
             info,
             (own, up_own, far_own, down_own),
             (taken, up_taken, far_taken, down_taken),
@@ -336,14 +330,16 @@
             qx_other,
             ahead,
         )
-        from_below = shift_y(plus, 1)
-        from_above = shift_y(minus, -1)
-        late_p = (late_p.astype(f32) + from_below[0].astype(f32)).astype(bf16)
-        late_m = (late_m.astype(f32) + from_above[1].astype(f32)).astype(bf16)
+        below_far = shift_y(far_p, 1)
+        above_far = shift_y(far_m, -1)
+        below_near = shift_y(near_p, 1)
+        above_near = shift_y(near_m, -1)
+        late_p = (late_p.astype(f32) + below_far.astype(f32)).astype(bf16)
+        late_m = (late_m.astype(f32) + above_far.astype(f32)).astype(bf16)
         got_p = shift_y(late_p, 1)
         got_m = shift_y(late_m, -1)
-        sum_first = mine[0].astype(f32) + got_p.astype(f32) + from_above[0].astype(f32)
-        sum_second = mine[1].astype(f32) + from_below[1].astype(f32) + got_m.astype(f32)
+        sum_first = mine[0].astype(f32) + got_p.astype(f32) + above_near.astype(f32)
+        sum_second = mine[1].astype(f32) + below_near.astype(f32) + got_m.astype(f32)
         near = jnp.stack([sum_first[:, :head_cols], sum_second[:, :head_cols]])
         other = jnp.stack([sum_first[:, head_cols:], sum_second[:, head_cols:]])
         got = swap_xl(jnp.where(same, other, near).astype(bf16))
@@ -361,13 +357,15 @@
     far = gather_x(jnp.where(xl == 0, blocks[:, :, 1], blocks[:, :, 0]))
     near = jnp.where(xl == 0, blocks[:, :, 0], blocks[:, :, 1])
     near = jnp.where(same, near, cross_x(near))
-    flipped = cross_x(narrow)
+    flipped = []
+    for value in done:
+        flipped.append(cross_x(value.astype(bf16)))
     both = jnp.stack([near, far])
     parts = [lax.dynamic_index_in_dim(both, z, 2, False)]
     for k in range(1, NZ):
         parts.append(shift_z(lax.dynamic_index_in_dim(both, (z + k) & (NZ - 1), 2, False), k))
     facts = jnp.stack([z, xh, same.astype(z.dtype)]).astype(jnp.int32)
-    return finish(facts, all_squares, parts, base, grads, flipped, ahead)
+    return finish(facts, all_squares, parts, base, grads, jnp.concatenate(flipped, axis=1), ahead)
 
 
 def solution(mesh):

time: 192 us -> 201 us (1.047)
  local copies, waits for them, and re-layouts: 2.46 us -> 18.7 us
  waiting for transfers between devices: 81.5 us -> 72.3 us
  starting transfers between devices: 62.2 us -> 67 us
  other arithmetic: 18.5 us -> 14.6 us
    unnamed x35 -> x41, local copies, waits for them, and re-layouts: 0.77 us -> 17 us
    ppermute x34 -> x39, waiting for transfers between devices: 56.9 us -> 50.6 us  [permute(): return lax.ppermute(value, BOTH, pairs)]
    ppermute x34 -> x39, starting transfers between devices: 53 us -> 58.7 us  [permute(): return lax.ppermute(value, BOTH, pairs)]
    all_to_all x1, waiting for transfers between devices: 23 us -> 18.8 us  [step(): lax.all_to_all(ahead, 'head', split_axis=0, concat_axis=0, tiled=True)]
    add x2, other arithmetic: 2.6 us -> 0.5 us  [step(): sum_first = mine[0].astype(f32) + got_p.astype(f32) + above_near.astype(f32)]
  transfers between devices with their start and end apart: 36 -> 41, of which waited for: 14 -> 16; matrix products, arithmetic and copies ran while one was open for 10% -> 8% of each run, Pallas kernels for 12% -> 12%
where the time goes in v1:
time: 201 us; the launch traced here: 199 us
  waiting for transfers between devices  72.3 us (36%)
  starting transfers between devices  67 us (33%)
  Pallas kernels  25.7 us (13%)
  local copies, waits for them, and re-layouts  18.7 us (9%)
  other arithmetic  14.6 us (7%)
    ppermute x39, starting transfers between devices, permute(): return lax.ppermute(value, BOTH, pairs)  58.7 us
    ppermute x39, waiting for transfers between devices, permute(): return lax.ppermute(value, BOTH, pairs)  50.6 us
    pallas_call x2, Pallas kernels, product(): pl.pallas_call(product_kernel, in_specs=[smem] * 3 + [anywhere] * 13, out...  21.2 us
    all_to_all x1, waiting for transfers between devices, step(): lax.all_to_all(ahead, 'head', split_axis=0, concat_axis=0, tiled=True)  18.8 us
    unnamed x41, local copies, waits for them, and re-layouts  17 us
    reduce_sum x1, other arithmetic, step(): jnp.sum(band_coefs.astype(f32)[:, None, None] * noise_history.astype(f32)...  7.3 us
    all_to_all x1, starting transfers between devices, step(): lax.all_to_all(jnp.broadcast_to(lanes, (count, 256)), BOTH, 0, 0, tiled=T...  4.87 us
  transfers between devices with their start and end apart: 41, of which 16 were waited for; matrix products, arithmetic and copies ran while one was open for 8% of the time, Pallas kernels for 12%

profile of v1, /device:TPU:0, one launch (start us, length us, event | category | flops | bytes accessed | tf_op | source)
XLA Modules:
  0.0 199.2 jit_solution(6329351163352415763)
XLA Ops:
  0.6 3.2 %collective-permute-start.8 = (bf16[2048,512]{1,0:T(8,128)(2,1)}, bf16[2048,512]{1,0:T(8,128)(2,1)}, u32[]{:S(2)}, u32[]{:S(2)}) collective-permute-start(bf16[2048,512]{1,0:T(8,128)(2,1)} %refs_8_.3), channel_id=1, source_target_pairs={{0,1},{1,0},{2,3},{3,2},{4,5},{5,4},{6,7},{7,6},{8,9},{9,8},{10,11... | collective-permute-start | bytes 6291464 | tf_op jit(solution)/shard_map/ppermute | solution.py:34
  3.8 2.9 %turn.1 = (bf16[144,2048]{1,0:T(8,128)(2,1)}, bf16[144,2048]{1,0:T(8,128)(2,1)}, bf16[112,2048]{1,0:T(8,128)(2,1)}, bf16[112,2048]{1,0:T(8,128)(2,1)}) custom-call(s32[1]{0:T(128)} %bitcast.5.core, bf16[2048,512]{1,0:T(8,128)(2,1)} %give.1, bf16[2048,512]{1,0:T(8,128)(2,1)} %give.1), custom_call_target="tpu_custom_call" | custom-call | bytes 4194304 | tf_op jit(solution)/shard_map/turn/pallas_call | solution.py:91
  12.2 2.2 %collective-permute-start.20 = (bf16[112,2048]{1,0:T(8,128)(2,1)}, bf16[112,2048]{1,0:T(8,128)(2,1)S(1)}, u32[]{:S(2)}, u32[]{:S(2)}) collective-permute-start(bf16[112,2048]{1,0:T(8,128)(2,1)} %get-tuple-element.29.refs_0_), channel_id=1, source_target_pairs={{0,6},{1,7},{2,0},{3,1},{4,2},{5,3},{6,4},{7,5},{8,14},{9,15},{10,... | collective-permute-start | bytes 1376264 | tf_op jit(solution)/shard_map/ppermute | solution.py:34
  14.4 7.9 %collective-permute-done.18.refs_1_ = bf16[112,2048]{1,0:T(8,128)(2,1)S(1)} collective-permute-done((bf16[112,2048]{1,0:T(8,128)(2,1)}, bf16[112,2048]{1,0:T(8,128)(2,1)S(1)}, u32[]{:S(2)}, u32[]{:S(2)}) %collective-permute-start.18) | collective-permute-done | bytes 458784 | tf_op jit(solution)/shard_map/ppermute | solution.py:34
  22.2 2.9 %collective-permute-done.20.refs_3_ = bf16[112,2048]{1,0:T(8,128)(2,1)S(1)} collective-permute-done((bf16[112,2048]{1,0:T(8,128)(2,1)}, bf16[112,2048]{1,0:T(8,128)(2,1)S(1)}, u32[]{:S(2)}, u32[]{:S(2)}) %collective-permute-start.20) | collective-permute-done | bytes 458784 | tf_op jit(solution)/shard_map/ppermute | solution.py:34
  25.9 3.4 %collective-permute-start.23 = (bf16[112,2048]{1,0:T(8,128)(2,1)S(1)}, bf16[112,2048]{1,0:T(8,128)(2,1)S(1)}, u32[]{:S(2)}, u32[]{:S(2)}) collective-permute-start(bf16[112,2048]{1,0:T(8,128)(2,1)S(1)} %collective-permute-done.21.refs_4_), channel_id=1, source_target_pairs={{0,6},{1,7},{2,0},{3,1},{4,2},{5,3},{6,4},{7,5},{8,14},{9,15},{10,... | collective-permute-start | bytes 1376264 | tf_op jit(solution)/shard_map/ppermute | solution.py:34
  30.0 9.9 %collective-permute-done.1.refs_1_ = bf16[144,2048]{1,0:T(8,128)(2,1)S(1)} collective-permute-done((bf16[144,2048]{1,0:T(8,128)(2,1)}, bf16[144,2048]{1,0:T(8,128)(2,1)S(1)}, u32[]{:S(2)}, u32[]{:S(2)}) %collective-permute-start.1) | collective-permute-done | bytes 589856 | tf_op jit(solution)/shard_map/ppermute | solution.py:34
  39.9 3.2 %collective-permute-start.6 = (bf16[144,2048]{1,0:T(8,128)(2,1)S(1)}, bf16[144,2048]{1,0:T(8,128)(2,1)}, u32[]{:S(2)}, u32[]{:S(2)}) collective-permute-start(bf16[144,2048]{1,0:T(8,128)(2,1)S(1)} %collective-permute-done.4.refs_4_), channel_id=1, source_target_pairs={{0,6},{1,7},{2,0},{3,1},{4,2},{5,3},{6,4},{7,5},{8,14},{9,15},{10,... | collective-permute-start | bytes 1769480 | tf_op jit(solution)/shard_map/ppermute | solution.py:34
  43.1 6.6 %collective-permute-done.19.refs_2_ = bf16[112,2048]{1,0:T(8,128)(2,1)S(1)} collective-permute-done((bf16[112,2048]{1,0:T(8,128)(2,1)S(1)}, bf16[112,2048]{1,0:T(8,128)(2,1)S(1)}, u32[]{:S(2)}, u32[]{:S(2)}) %collective-permute-start.19) | collective-permute-done | bytes 458784 | tf_op jit(solution)/shard_map/ppermute | solution.py:34
  51.0 7.3 %multiply_reduce_fusion = f32[32,4096]{1,0:T(8,128)S(1)} fusion(bf16[64,32,4096]{2,1,0:T(8,128)(2,1)} %param.10, f32[64]{0:T(128)S(1)} %convert_element_type.123), kind=kLoop, calls=%fused_computation | loop fusion | flops 25034752 | bytes 17301760 | tf_op jit(solution)/shard_map/reduce_sum | solution.py:304
  59.3 2.9 %collective-permute-start.3 = (bf16[144,2048]{1,0:T(8,128)(2,1)S(1)}, bf16[144,2048]{1,0:T(8,128)(2,1)}, u32[]{:S(2)}, u32[]{:S(2)}) collective-permute-start(bf16[144,2048]{1,0:T(8,128)(2,1)S(1)} %copy-done.5), channel_id=1, source_target_pairs={{0,6},{1,7},{2,0},{3,1},{4,2},{5,3},{6,4},{7,5},{8,14},{9,15},{10,... | collective-permute-start | bytes 1769480 | tf_op jit(solution)/shard_map/ppermute | solution.py:34
  62.2 3.0 %collective-permute-done.24.refs_6_ = bf16[112,2048]{1,0:T(8,128)(2,1)S(1)} collective-permute-done((bf16[112,2048]{1,0:T(8,128)(2,1)S(1)}, bf16[112,2048]{1,0:T(8,128)(2,1)S(1)}, u32[]{:S(2)}, u32[]{:S(2)}) %collective-permute-start.24) | collective-permute-done | bytes 458784 | tf_op jit(solution)/shard_map/ppermute | solution.py:34
  67.4 3.7 %collective-permute-start.7 = (bf16[144,2048]{1,0:T(8,128)(2,1)}, bf16[144,2048]{1,0:T(8,128)(2,1)}, u32[]{:S(2)}, u32[]{:S(2)}) collective-permute-start(bf16[144,2048]{1,0:T(8,128)(2,1)} %collective-permute-done.6.refs_7_), channel_id=1, source_target_pairs={{0,6},{1,7},{2,0},{3,1},{4,2},{5,3},{6,4},{7,5},{8,14},{9,15},{10,... | collective-permute-start | bytes 1769480 | tf_op jit(solution)/shard_map/ppermute | solution.py:34
  71.9 3.4 %all-to-all-start = ((bf16[8,32,512]{2,1,0:T(8,128)(2,1)}), bf16[8,32,512]{2,1,0:T(8,128)(2,1)S(1)}, u32[]{:S(2)}, u32[]{:S(2)}) async-start(bf16[8,32,512]{2,1,0:T(8,128)(2,1)} %bitcast.89), calls=%async_computation | async-start | bytes 524288 | tf_op jit(solution)/shard_map/all_to_all | solution.py:309
  75.4 18.8 %all-to-all-done = bf16[8,32,512]{2,1,0:T(8,128)(2,1)S(1)} async-done(((bf16[8,32,512]{2,1,0:T(8,128)(2,1)}), bf16[8,32,512]{2,1,0:T(8,128)(2,1)S(1)}, u32[]{:S(2)}, u32[]{:S(2)}) %all-to-all-start) | async-done | bytes 262176 | tf_op jit(solution)/shard_map/all_to_all | solution.py:309
  103.6 11.5 %product.3 = (bf16[112,1024]{1,0:T(8,128)(2,1)S(1)}, bf16[112,1024]{1,0:T(8,128)(2,1)S(1)}, bf16[112,1024]{1,0:T(8,128)(2,1)S(1)}, bf16[112,1024]{1,0:T(8,128)(2...) custom-call(s32[1]{0:T(128)} %bitcast.3.count_a, ...), custom_call_target="tpu_custom_call" | custom-call | flops 3758096384 | bytes 13893632 | tf_op jit(solution)/shard_map/product/pallas_call | solution.py:217
  115.1 3.1 %collective-permute-start.29 = (bf16[112,1024]{1,0:T(8,128)(2,1)S(1)}, bf16[112,1024]{1,0:T(8,128)(2,1)S(1)}, u32[]{:S(2)}, u32[]{:S(2)}) collective-permute-start(bf16[112,1024]{1,0:T(8,128)(2,1)S(1)} %get-tuple-element.37), channel_id=1, source_target_pairs={{0,96},{1,97},{2,98},{3,99},{4,100},{5,101},{6,102},{7,103},{8,104... | collective-permute-start | bytes 688136 | tf_op jit(solution)/shard_map/ppermute | solution.py:34
  118.2 3.2 %collective-permute-start.27 = (bf16[112,1024]{1,0:T(8,128)(2,1)S(1)}, bf16[112,1024]{1,0:T(8,128)(2,1)S(1)}, u32[]{:S(2)}, u32[]{:S(2)}) collective-permute-start(bf16[112,1024]{1,0:T(8,128)(2,1)S(1)} %get-tuple-element.34), channel_id=1, source_target_pairs={{0,96},{1,97},{2,98},{3,99},{4,100},{5,101},{6,102},{7,103},{8,104... | collective-permute-start | bytes 688136 | tf_op jit(solution)/shard_map/ppermute | solution.py:34
  124.6 9.7 %product.2 = (bf16[144,1024]{1,0:T(8,128)(2,1)S(1)}, bf16[144,1024]{1,0:T(8,128)(2,1)S(1)}, bf16[144,1024]{1,0:T(8,128)(2,1)S(1)}, bf16[144,1024]{1,0:T(8,128)(2...) custom-call(s32[1]{0:T(128)} %bitcast.3.count_a, ...), custom_call_target="tpu_custom_call" | custom-call | flops 4831838208 | bytes 15466496 | tf_op jit(solution)/shard_map/product/pallas_call | solution.py:217
  134.3 3.3 %collective-permute-start.15 = (bf16[144,1024]{1,0:T(8,128)(2,1)S(1)}, bf16[144,1024]{1,0:T(8,128)(2,1)S(1)}, u32[]{:S(2)}, u32[]{:S(2)}) collective-permute-start(bf16[144,1024]{1,0:T(8,128)(2,1)S(1)} %get-tuple-element.28), channel_id=1, source_target_pairs={{0,96},{1,97},{2,98},{3,99},{4,100},{5,101},{6,102},{7,103},{8,104... | collective-permute-start | bytes 884744 | tf_op jit(solution)/shard_map/ppermute | solution.py:34
  137.7 3.3 %collective-permute-start.13 = (bf16[144,1024]{1,0:T(8,128)(2,1)S(1)}, bf16[144,1024]{1,0:T(8,128)(2,1)S(1)}, u32[]{:S(2)}, u32[]{:S(2)}) collective-permute-start(bf16[144,1024]{1,0:T(8,128)(2,1)S(1)} %get-tuple-element.25), channel_id=1, source_target_pairs={{0,96},{1,97},{2,98},{3,99},{4,100},{5,101},{6,102},{7,103},{8,104... | collective-permute-start | bytes 884744 | tf_op jit(solution)/shard_map/ppermute | solution.py:34
  141.1 4.0 %collective-permute-done.15 = bf16[144,1024]{1,0:T(8,128)(2,1)S(1)} collective-permute-done((bf16[144,1024]{1,0:T(8,128)(2,1)S(1)}, bf16[144,1024]{1,0:T(8,128)(2,1)S(1)}, u32[]{:S(2)}, u32[]{:S(2)}) %collective-permute-start.15) | collective-permute-done | bytes 294944 | tf_op jit(solution)/shard_map/ppermute | solution.py:34
  145.0 3.7 %collective-permute-start.30 = (bf16[112,1024]{1,0:T(8,128)(2,1)S(1)}, bf16[112,1024]{1,0:T(8,128)(2,1)S(1)}, u32[]{:S(2)}, u32[]{:S(2)}) collective-permute-start(bf16[112,1024]{1,0:T(8,128)(2,1)S(1)} %add_convert_fusion.3), channel_id=1, source_target_pairs={{0,96},{1,97},{2,98},{3,99},{4,100},{5,101},{6,102},{7,103},{8,104... | collective-permute-start | bytes 688136 | tf_op jit(solution)/shard_map/ppermute | solution.py:34
  149.1 3.3 %collective-permute-start.16 = (bf16[144,1024]{1,0:T(8,128)(2,1)S(1)}, bf16[144,1024]{1,0:T(8,128)(2,1)S(1)}, u32[]{:S(2)}, u32[]{:S(2)}) collective-permute-start(bf16[144,1024]{1,0:T(8,128)(2,1)S(1)} %add_convert_fusion), channel_id=1, source_target_pairs={{0,96},{1,97},{2,98},{3,99},{4,100},{5,101},{6,102},{7,103},{8,104... | collective-permute-start | bytes 884744 | tf_op jit(solution)/shard_map/ppermute | solution.py:34
  152.4 3.9 %collective-permute-done.30 = bf16[112,1024]{1,0:T(8,128)(2,1)S(1)} collective-permute-done((bf16[112,1024]{1,0:T(8,128)(2,1)S(1)}, bf16[112,1024]{1,0:T(8,128)(2,1)S(1)}, u32[]{:S(2)}, u32[]{:S(2)}) %collective-permute-start.30) | collective-permute-done | bytes 229408 | tf_op jit(solution)/shard_map/ppermute | solution.py:34
  156.9 2.2 %collective-permute-start.31 = (bf16[2,112,512]{2,1,0:T(8,128)(2,1)S(1)}, bf16[2,112,512]{2,1,0:T(8,128)(2,1)S(1)}, u32[]{:S(2)}, u32[]{:S(2)}) collective-permute-start(bf16[2,112,512]{2,1,0:T(8,128)(2,1)S(1)} %select_convert_fusion.1), channel_id=1, source_target_pairs={{0,16},{1,17},{2,18},{3,19},{4,20},{5,21},{6,22},{7,23},{8,24},{9,... | collective-permute-start | bytes 688136 | tf_op jit(solution)/shard_map/ppermute | solution.py:34
  159.1 3.3 %collective-permute-done.14 = bf16[144,1024]{1,0:T(8,128)(2,1)S(1)} collective-permute-done((bf16[144,1024]{1,0:T(8,128)(2,1)S(1)}, bf16[144,1024]{1,0:T(8,128)(2,1)S(1)}, u32[]{:S(2)}, u32[]{:S(2)}) %collective-permute-start.14) | collective-permute-done | bytes 294944 | tf_op jit(solution)/shard_map/ppermute | solution.py:34
  162.4 3.2 %collective-permute-done.12 = bf16[144,1024]{1,0:T(8,128)(2,1)S(1)} collective-permute-done((bf16[144,1024]{1,0:T(8,128)(2,1)S(1)}, bf16[144,1024]{1,0:T(8,128)(2,1)S(1)}, u32[]{:S(2)}, u32[]{:S(2)}) %collective-permute-start.12) | collective-permute-done | bytes 294944 | tf_op jit(solution)/shard_map/ppermute | solution.py:34
  173.9 2.8 %collective-permute-start.32 = (bf16[2,4,32,512]{3,2,1,0:T(8,128)(2,1)S(1)}, bf16[2,4,32,512]{3,2,1,0:T(8,128)(2,1)S(1)}, u32[]{:S(2)}, u32[]{:S(2)}) collective-permute-start(bf16[2,4,32,512]{3,2,1,0:T(8,128)(2,1)S(1)} %fusion.5), channel_id=1, source_target_pairs={{0,17},{1,16},{2,19},{3,18},{4,21},{5,20},{6,23},{7,22},{8,25},{9,... | collective-permute-start | bytes 786440 | tf_op jit(solution)/shard_map/ppermute | solution.py:34
  180.0 4.9 %all-to-all-start.1 = ((f32[128,1,256]{2,1,0:T(1,128)}), f32[128,1,256]{2,1,0:T(1,128)S(1)}, u32[]{:S(2)}, u32[]{:S(2)}) async-start(f32[128,1,256]{2,1,0:T(1,128)} %broadcast_in_dim.13), calls=%async_computation.1 | async-start | bytes 262144 | tf_op jit(solution)/shard_map/all_to_all | solution.py:353
  186.8 3.2 %collective-permute-start.35 = (bf16[2,2,32,512]{3,2,1,0:T(8,128)(2,1)}, bf16[2,2,32,512]{3,2,1,0:T(8,128)(2,1)S(1)}, u32[]{:S(2)}, u32[]{:S(2)}) collective-permute-start(bf16[2,2,32,512]{3,2,1,0:T(8,128)(2,1)} %get-tuple-element.53), channel_id=1, source_target_pairs={{0,4},{1,5},{2,6},{3,7},{4,0},{5,1},{6,2},{7,3},{8,12},{9,13},{10,... | collective-permute-start | bytes 393224 | tf_op jit(solution)/shard_map/ppermute | solution.py:34
  191.3 2.9 %all-to-all-done.1 = f32[128,1,256]{2,1,0:T(1,128)S(1)} async-done(((f32[128,1,256]{2,1,0:T(1,128)}), f32[128,1,256]{2,1,0:T(1,128)S(1)}, u32[]{:S(2)}, u32[]{:S(2)}) %all-to-all-start.1) | async-done | bytes 131104 | tf_op jit(solution)/shard_map/all_to_all | solution.py:353
  (125 shorter events, 45.6 us)
Async XLA Ops:
  0.6 50.4 %collective-permute-start.8 = (bf16[2048,512]{1,0:T(8,128)(2,1)}, bf16[2048,512]{1,0:T(8,128)(2,1)}, u32[]{:S(2)}, u32[]{:S(2)}) collective-permute-start(bf16[2048,512]{1,0:T(8,128)(2,1)} %refs_8_.3), channel_id=1, source_target_pairs={{0,1},{1,0},{2,3},{3,2},{4,5},{5,4},{6,7},{7,6},{8,9},{9,8},{10,11... | collective-permute-start | bytes 6291464 | tf_op jit(solution)/shard_map/ppermute | solution.py:34
  6.8 15.4 %collective-permute-start.18 = (bf16[112,2048]{1,0:T(8,128)(2,1)}, bf16[112,2048]{1,0:T(8,128)(2,1)S(1)}, u32[]{:S(2)}, u32[]{:S(2)}) collective-permute-start(bf16[112,2048]{1,0:T(8,128)(2,1)} %get-tuple-element.29.refs_0_), channel_id=1, source_target_pairs={{0,2},{1,3},{2,4},{3,5},{4,6},{5,7},{6,0},{7,1},{8,10},{9,11},{10,... | collective-permute-start | bytes 1376264 | tf_op jit(solution)/shard_map/ppermute | solution.py:34
  8.8 20.6 %collective-permute-start.4 = (bf16[144,2048]{1,0:T(8,128)(2,1)}, bf16[144,2048]{1,0:T(8,128)(2,1)S(1)}, u32[]{:S(2)}, u32[]{:S(2)}) collective-permute-start(bf16[144,2048]{1,0:T(8,128)(2,1)} %get-tuple-element.21), channel_id=1, source_target_pairs={{0,8},{1,9},{2,10},{3,11},{4,12},{5,13},{6,14},{7,15},{8,0},{9,1},... | collective-permute-start | bytes 1769480 | tf_op jit(solution)/shard_map/ppermute | solution.py:34
  11.8 54.2 %collective-permute-start.9 = (bf16[2048,512]{1,0:T(8,128)(2,1)}, bf16[2048,512]{1,0:T(8,128)(2,1)S(1)}, u32[]{:S(2)}, u32[]{:S(2)}) collective-permute-start(bf16[2048,512]{1,0:T(8,128)(2,1)} %refs_8_.3), channel_id=1, source_target_pairs={{0,8},{1,9},{2,10},{3,11},{4,12},{5,13},{6,14},{7,15},{8,0},{9,1},... | collective-permute-start | bytes 6291464 | tf_op jit(solution)/shard_map/ppermute | solution.py:34
  12.2 13.0 %collective-permute-start.20 = (bf16[112,2048]{1,0:T(8,128)(2,1)}, bf16[112,2048]{1,0:T(8,128)(2,1)S(1)}, u32[]{:S(2)}, u32[]{:S(2)}) collective-permute-start(bf16[112,2048]{1,0:T(8,128)(2,1)} %get-tuple-element.29.refs_0_), channel_id=1, source_target_pairs={{0,6},{1,7},{2,0},{3,1},{4,2},{5,3},{6,4},{7,5},{8,14},{9,15},{10,... | collective-permute-start | bytes 1376264 | tf_op jit(solution)/shard_map/ppermute | solution.py:34
  22.2 17.6 %collective-permute-start.1 = (bf16[144,2048]{1,0:T(8,128)(2,1)}, bf16[144,2048]{1,0:T(8,128)(2,1)S(1)}, u32[]{:S(2)}, u32[]{:S(2)}) collective-permute-start(bf16[144,2048]{1,0:T(8,128)(2,1)} %get-tuple-element.20.refs_0_), channel_id=1, source_target_pairs={{0,2},{1,3},{2,4},{3,5},{4,6},{5,7},{6,0},{7,1},{8,10},{9,11},{10,... | collective-permute-start | bytes 1769480 | tf_op jit(solution)/shard_map/ppermute | solution.py:34
  25.9 13.9 %collective-permute-start.23 = (bf16[112,2048]{1,0:T(8,128)(2,1)S(1)}, bf16[112,2048]{1,0:T(8,128)(2,1)S(1)}, u32[]{:S(2)}, u32[]{:S(2)}) collective-permute-start(bf16[112,2048]{1,0:T(8,128)(2,1)S(1)} %collective-permute-done.21.refs_4_), channel_id=1, source_target_pairs={{0,6},{1,7},{2,0},{3,1},{4,2},{5,3},{6,4},{7,5},{8,14},{9,15},{10,... | collective-permute-start | bytes 1376264 | tf_op jit(solution)/shard_map/ppermute | solution.py:34
  29.3 20.3 %collective-permute-start.19 = (bf16[112,2048]{1,0:T(8,128)(2,1)S(1)}, bf16[112,2048]{1,0:T(8,128)(2,1)S(1)}, u32[]{:S(2)}, u32[]{:S(2)}) collective-permute-start(bf16[112,2048]{1,0:T(8,128)(2,1)S(1)} %collective-permute-done.18.refs_1_), channel_id=1, source_target_pairs={{0,2},{1,3},{2,4},{3,5},{4,6},{5,7},{6,0},{7,1},{8,10},{9,11},{10,... | collective-permute-start | bytes 1376264 | tf_op jit(solution)/shard_map/ppermute | solution.py:34
  39.9 18.6 %collective-permute-start.22 = (bf16[112,2048]{1,0:T(8,128)(2,1)S(1)}, bf16[112,2048]{1,0:T(8,128)(2,1)S(1)}, u32[]{:S(2)}, u32[]{:S(2)}) collective-permute-start(bf16[112,2048]{1,0:T(8,128)(2,1)S(1)} %collective-permute-done.21.refs_4_), channel_id=1, source_target_pairs={{0,2},{1,3},{2,4},{3,5},{4,6},{5,7},{6,0},{7,1},{8,10},{9,11},{10,... | collective-permute-start | bytes 1376264 | tf_op jit(solution)/shard_map/ppermute | solution.py:34
  39.9 22.3 %collective-permute-start.6 = (bf16[144,2048]{1,0:T(8,128)(2,1)S(1)}, bf16[144,2048]{1,0:T(8,128)(2,1)}, u32[]{:S(2)}, u32[]{:S(2)}) collective-permute-start(bf16[144,2048]{1,0:T(8,128)(2,1)S(1)} %collective-permute-done.4.refs_4_), channel_id=1, source_target_pairs={{0,6},{1,7},{2,0},{3,1},{4,2},{5,3},{6,4},{7,5},{8,14},{9,15},{10,... | collective-permute-start | bytes 1769480 | tf_op jit(solution)/shard_map/ppermute | solution.py:34
  50.5 14.7 %collective-permute-start.24 = (bf16[112,2048]{1,0:T(8,128)(2,1)S(1)}, bf16[112,2048]{1,0:T(8,128)(2,1)S(1)}, u32[]{:S(2)}, u32[]{:S(2)}) collective-permute-start(bf16[112,2048]{1,0:T(8,128)(2,1)S(1)} %collective-permute-done.23.refs_7_), channel_id=1, source_target_pairs={{0,6},{1,7},{2,0},{3,1},{4,2},{5,3},{6,4},{7,5},{8,14},{9,15},{10,... | collective-permute-start | bytes 1376264 | tf_op jit(solution)/shard_map/ppermute | solution.py:34
  51.0 43.3 %collective-permute-start.10 = (bf16[2048,512]{1,0:T(8,128)(2,1)}, bf16[2048,512]{1,0:T(8,128)(2,1)}, u32[]{:S(2)}, u32[]{:S(2)}) collective-permute-start(bf16[2048,512]{1,0:T(8,128)(2,1)} %collective-permute-done.8.refs_9_), channel_id=1, source_target_pairs={{0,8},{1,9},{2,10},{3,11},{4,12},{5,13},{6,14},{7,15},{8,0},{9,1},... | collective-permute-start | bytes 6291464 | tf_op jit(solution)/shard_map/ppermute | solution.py:34
  59.3 58.9 %collective-permute-start.3 = (bf16[144,2048]{1,0:T(8,128)(2,1)S(1)}, bf16[144,2048]{1,0:T(8,128)(2,1)}, u32[]{:S(2)}, u32[]{:S(2)}) collective-permute-start(bf16[144,2048]{1,0:T(8,128)(2,1)S(1)} %copy-done.5), channel_id=1, source_target_pairs={{0,6},{1,7},{2,0},{3,1},{4,2},{5,3},{6,4},{7,5},{8,14},{9,15},{10,... | collective-permute-start | bytes 1769480 | tf_op jit(solution)/shard_map/ppermute | solution.py:34
  62.2 59.3 %collective-permute-start.5 = (bf16[144,2048]{1,0:T(8,128)(2,1)S(1)}, bf16[144,2048]{1,0:T(8,128)(2,1)}, u32[]{:S(2)}, u32[]{:S(2)}) collective-permute-start(bf16[144,2048]{1,0:T(8,128)(2,1)S(1)} %collective-permute-done.4.refs_4_), channel_id=1, source_target_pairs={{0,2},{1,3},{2,4},{3,5},{4,6},{5,7},{6,0},{7,1},{8,10},{9,11},{10,... | collective-permute-start | bytes 1769480 | tf_op jit(solution)/shard_map/ppermute | solution.py:34
  66.0 52.2 %collective-permute-start.2 = (bf16[144,2048]{1,0:T(8,128)(2,1)S(1)}, bf16[144,2048]{1,0:T(8,128)(2,1)}, u32[]{:S(2)}, u32[]{:S(2)}) collective-permute-start(bf16[144,2048]{1,0:T(8,128)(2,1)S(1)} %collective-permute-done.1.refs_1_), channel_id=1, source_target_pairs={{0,2},{1,3},{2,4},{3,5},{4,6},{5,7},{6,0},{7,1},{8,10},{9,11},{10,... | collective-permute-start | bytes 1769480 | tf_op jit(solution)/shard_map/ppermute | solution.py:34
  67.4 54.1 %collective-permute-start.7 = (bf16[144,2048]{1,0:T(8,128)(2,1)}, bf16[144,2048]{1,0:T(8,128)(2,1)}, u32[]{:S(2)}, u32[]{:S(2)}) collective-permute-start(bf16[144,2048]{1,0:T(8,128)(2,1)} %collective-permute-done.6.refs_7_), channel_id=1, source_target_pairs={{0,6},{1,7},{2,0},{3,1},{4,2},{5,3},{6,4},{7,5},{8,14},{9,15},{10,... | collective-permute-start | bytes 1769480 | tf_op jit(solution)/shard_map/ppermute | solution.py:34
  71.9 22.4 %all-to-all-start = ((bf16[8,32,512]{2,1,0:T(8,128)(2,1)}), bf16[8,32,512]{2,1,0:T(8,128)(2,1)S(1)}, u32[]{:S(2)}, u32[]{:S(2)}) async-start(bf16[8,32,512]{2,1,0:T(8,128)(2,1)} %bitcast.89), calls=%async_computation | async-start | bytes 524288 | tf_op jit(solution)/shard_map/all_to_all | solution.py:309
  115.1 22.6 %collective-permute-start.29 = (bf16[112,1024]{1,0:T(8,128)(2,1)S(1)}, bf16[112,1024]{1,0:T(8,128)(2,1)S(1)}, u32[]{:S(2)}, u32[]{:S(2)}) collective-permute-start(bf16[112,1024]{1,0:T(8,128)(2,1)S(1)} %get-tuple-element.37), channel_id=1, source_target_pairs={{0,96},{1,97},{2,98},{3,99},{4,100},{5,101},{6,102},{7,103},{8,104... | collective-permute-start | bytes 688136 | tf_op jit(solution)/shard_map/ppermute | solution.py:34
  118.2 19.5 %collective-permute-start.25 = (bf16[112,1024]{1,0:T(8,128)(2,1)S(1)}, bf16[112,1024]{1,0:T(8,128)(2,1)S(1)}, u32[]{:S(2)}, u32[]{:S(2)}) collective-permute-start(bf16[112,1024]{1,0:T(8,128)(2,1)S(1)} %get-tuple-element.33), channel_id=1, source_target_pairs={{0,32},{1,33},{2,34},{3,35},{4,36},{5,37},{6,38},{7,39},{8,40},{9,... | collective-permute-start | bytes 688136 | tf_op jit(solution)/shard_map/ppermute | solution.py:34
  118.2 30.8 %collective-permute-start.27 = (bf16[112,1024]{1,0:T(8,128)(2,1)S(1)}, bf16[112,1024]{1,0:T(8,128)(2,1)S(1)}, u32[]{:S(2)}, u32[]{:S(2)}) collective-permute-start(bf16[112,1024]{1,0:T(8,128)(2,1)S(1)} %get-tuple-element.34), channel_id=1, source_target_pairs={{0,96},{1,97},{2,98},{3,99},{4,100},{5,101},{6,102},{7,103},{8,104... | collective-permute-start | bytes 688136 | tf_op jit(solution)/shard_map/ppermute | solution.py:34
  121.4 27.7 %collective-permute-start.28 = (bf16[112,1024]{1,0:T(8,128)(2,1)S(1)}, bf16[112,1024]{1,0:T(8,128)(2,1)S(1)}, u32[]{:S(2)}, u32[]{:S(2)}) collective-permute-start(bf16[112,1024]{1,0:T(8,128)(2,1)S(1)} %get-tuple-element.35), channel_id=1, source_target_pairs={{0,32},{1,33},{2,34},{3,35},{4,36},{5,37},{6,38},{7,39},{8,40},{9,... | collective-permute-start | bytes 688136 | tf_op jit(solution)/shard_map/ppermute | solution.py:34
  137.6 11.2 %collective-permute-start.11 = (bf16[144,1024]{1,0:T(8,128)(2,1)S(1)}, bf16[144,1024]{1,0:T(8,128)(2,1)S(1)}, u32[]{:S(2)}, u32[]{:S(2)}) collective-permute-start(bf16[144,1024]{1,0:T(8,128)(2,1)S(1)} %get-tuple-element.24), channel_id=1, source_target_pairs={{0,32},{1,33},{2,34},{3,35},{4,36},{5,37},{6,38},{7,39},{8,40},{9,... | collective-permute-start | bytes 884744 | tf_op jit(solution)/shard_map/ppermute | solution.py:34
  137.7 21.4 %collective-permute-start.13 = (bf16[144,1024]{1,0:T(8,128)(2,1)S(1)}, bf16[144,1024]{1,0:T(8,128)(2,1)S(1)}, u32[]{:S(2)}, u32[]{:S(2)}) collective-permute-start(bf16[144,1024]{1,0:T(8,128)(2,1)S(1)} %get-tuple-element.25), channel_id=1, source_target_pairs={{0,96},{1,97},{2,98},{3,99},{4,100},{5,101},{6,102},{7,103},{8,104... | collective-permute-start | bytes 884744 | tf_op jit(solution)/shard_map/ppermute | solution.py:34
  145.0 11.2 %collective-permute-start.30 = (bf16[112,1024]{1,0:T(8,128)(2,1)S(1)}, bf16[112,1024]{1,0:T(8,128)(2,1)S(1)}, u32[]{:S(2)}, u32[]{:S(2)}) collective-permute-start(bf16[112,1024]{1,0:T(8,128)(2,1)S(1)} %add_convert_fusion.3), channel_id=1, source_target_pairs={{0,96},{1,97},{2,98},{3,99},{4,100},{5,101},{6,102},{7,103},{8,104... | collective-permute-start | bytes 688136 | tf_op jit(solution)/shard_map/ppermute | solution.py:34
  149.0 13.4 %collective-permute-start.14 = (bf16[144,1024]{1,0:T(8,128)(2,1)S(1)}, bf16[144,1024]{1,0:T(8,128)(2,1)S(1)}, u32[]{:S(2)}, u32[]{:S(2)}) collective-permute-start(bf16[144,1024]{1,0:T(8,128)(2,1)S(1)} %get-tuple-element.26), channel_id=1, source_target_pairs={{0,32},{1,33},{2,34},{3,35},{4,36},{5,37},{6,38},{7,39},{8,40},{9,... | collective-permute-start | bytes 884744 | tf_op jit(solution)/shard_map/ppermute | solution.py:34
  149.1 13.4 %collective-permute-start.16 = (bf16[144,1024]{1,0:T(8,128)(2,1)S(1)}, bf16[144,1024]{1,0:T(8,128)(2,1)S(1)}, u32[]{:S(2)}, u32[]{:S(2)}) collective-permute-start(bf16[144,1024]{1,0:T(8,128)(2,1)S(1)} %add_convert_fusion), channel_id=1, source_target_pairs={{0,96},{1,97},{2,98},{3,99},{4,100},{5,101},{6,102},{7,103},{8,104... | collective-permute-start | bytes 884744 | tf_op jit(solution)/shard_map/ppermute | solution.py:34
  156.9 10.8 %collective-permute-start.31 = (bf16[2,112,512]{2,1,0:T(8,128)(2,1)S(1)}, bf16[2,112,512]{2,1,0:T(8,128)(2,1)S(1)}, u32[]{:S(2)}, u32[]{:S(2)}) collective-permute-start(bf16[2,112,512]{2,1,0:T(8,128)(2,1)S(1)} %select_convert_fusion.1), channel_id=1, source_target_pairs={{0,16},{1,17},{2,18},{3,19},{4,20},{5,21},{6,22},{7,23},{8,24},{9,... | collective-permute-start | bytes 688136 | tf_op jit(solution)/shard_map/ppermute | solution.py:34
  168.5 25.7 %collective-permute-start.38 = (bf16[2,112,512]{2,1,0:T(8,128)(2,1)}, bf16[2,112,512]{2,1,0:T(8,128)(2,1)}, u32[]{:S(2)}, u32[]{:S(2)}) collective-permute-start(bf16[2,112,512]{2,1,0:T(8,128)(2,1)} %get-tuple-element.40), channel_id=1, source_target_pairs={{0,17},{1,16},{2,19},{3,18},{4,21},{5,20},{6,23},{7,22},{8,25},{9,... | collective-permute-start | bytes 688136 | tf_op jit(solution)/shard_map/ppermute | solution.py:34
  173.9 11.0 %collective-permute-start.32 = (bf16[2,4,32,512]{3,2,1,0:T(8,128)(2,1)S(1)}, bf16[2,4,32,512]{3,2,1,0:T(8,128)(2,1)S(1)}, u32[]{:S(2)}, u32[]{:S(2)}) collective-permute-start(bf16[2,4,32,512]{3,2,1,0:T(8,128)(2,1)S(1)} %fusion.5), channel_id=1, source_target_pairs={{0,17},{1,16},{2,19},{3,18},{4,21},{5,20},{6,23},{7,22},{8,25},{9,... | collective-permute-start | bytes 786440 | tf_op jit(solution)/shard_map/ppermute | solution.py:34
  176.9 17.3 %collective-permute-start.37 = (bf16[2,144,512]{2,1,0:T(8,128)(2,1)}, bf16[2,144,512]{2,1,0:T(8,128)(2,1)}, u32[]{:S(2)}, u32[]{:S(2)}) collective-permute-start(bf16[2,144,512]{2,1,0:T(8,128)(2,1)} %get-tuple-element.38), channel_id=1, source_target_pairs={{0,17},{1,16},{2,19},{3,18},{4,21},{5,20},{6,23},{7,22},{8,25},{9,... | collective-permute-start | bytes 884744 | tf_op jit(solution)/shard_map/ppermute | solution.py:34
  180.0 14.2 %all-to-all-start.1 = ((f32[128,1,256]{2,1,0:T(1,128)}), f32[128,1,256]{2,1,0:T(1,128)S(1)}, u32[]{:S(2)}, u32[]{:S(2)}) async-start(f32[128,1,256]{2,1,0:T(1,128)} %broadcast_in_dim.13), calls=%async_computation.1 | async-start | bytes 262144 | tf_op jit(solution)/shard_map/all_to_all | solution.py:353
  186.8 10.7 %collective-permute-start.35 = (bf16[2,2,32,512]{3,2,1,0:T(8,128)(2,1)}, bf16[2,2,32,512]{3,2,1,0:T(8,128)(2,1)S(1)}, u32[]{:S(2)}, u32[]{:S(2)}) collective-permute-start(bf16[2,2,32,512]{3,2,1,0:T(8,128)(2,1)} %get-tuple-element.53), channel_id=1, source_target_pairs={{0,4},{1,5},{2,6},{3,7},{4,0},{5,1},{6,2},{7,3},{8,12},{9,13},{10,... | collective-permute-start | bytes 393224 | tf_op jit(solution)/shard_map/ppermute | solution.py:34
  (29 other events, 365.5 us)
